TPU v7x, 128 devices: a whole 4x4x4 slice. The times are simulated.
128 devices in a mesh: seq: 16 (over x, z_hi, core), head: 8 (over z_lo, y).
Axes of the slice: x: 4, y: 4, z: 4 (z_hi: 2, z_lo: 2; z = z_hi * 2 + z_lo), core: 2. Of those that a mesh axis runs over, the one named last changes fastest.
Arguments:
- hidden: bfloat16 [8192, 4096], P(('seq', 'head')), may hold values from -6 to 6
- masked: int32 [8192], P(('seq', 'head')), may hold values 0 or 1
- mask_embed: bfloat16 [4096], replicated, may hold values from -6 to 6
- in_gain: float32 [4096], replicated, may hold values from 0.5 to 1.5
- w_gate: bfloat16 [4096, 4096], P(None, 'head'), may hold values from -0.09375 to 0.09375
- w_value: bfloat16 [4096, 4096], P(None, 'head'), may hold values from -0.09375 to 0.09375
- w_step: bfloat16 [4096, 64], P(None, 'head'), may hold values from -0.09375 to 0.09375
- w_bc: bfloat16 [4096, 256], replicated, may hold values from -0.0078125 to 0.0078125
- dt_bias_forward: float32 [64], P('head'), may hold values from -1 to 1
- dt_bias_reverse: float32 [64], P('head'), may hold values from -1 to 1
- rate_forward: float32 [64], P('head'), as said below
- rate_reverse: float32 [64], P('head'), as said below
- skip_forward: float32 [64], P('head'), may hold values from 0.5 to 1.5
- skip_reverse: float32 [64], P('head'), may hold values from 0.5 to 1.5
- out_gain: float32 [4096], P('head'), may hold values from 0.1 to 1.9
- w_out: bfloat16 [4096, 4096], P('head'), may hold values from -0.09375 to 0.09375
Outputs:
- mixed: bfloat16 [8192, 4096], P(('seq', 'head'))
Inputs may be any that keep to these rules, and one draw needn't show every extreme that they name: `rate_forward`: positive decay rates of the 64 heads, each at most 0.05 a position. `rate_reverse`: positive decay rates of the 64 heads, each at most 0.05 a position.
All inputs are finite; a program needn't handle non-finite values. No bound on the sum of `masked` on one device may be relied on, other than what follows from the above.
Results may differ from a plain program's by a relative error of at most 0.014.
The roundings to bfloat16 on the way count: a program that leaves them out, or rounds other values in their place, can miss the bound.
Values may be sent and summed in bfloat16 or wider, within the bound.
No kernel may reach another device: no remote copies, remote signals or barrier semaphores. Data moves between devices by JAX's collectives and lax.ppermute only.
A program may use at most 128 MiB of HBM per device.

v0:
```python
import functools

import jax
import jax.numpy as jnp
from jax import lax
from jax.experimental import pallas as pl
from jax.experimental.pallas import tpu as pltpu
from jax.sharding import PartitionSpec as P


HEADS = 64
HEAD_DIM = 64
STATE = 128
BLOCK = 256
EPSILON = 1e-05
OWN = 8
ROWS = 512
PIECE = 64
WIDE = OWN * HEAD_DIM
PAY = STATE + 8

f32 = jnp.float32
bf16 = jnp.bfloat16

MASK = {"A": 1, "B": 3, "Z": 4}
CUT = {"A": (0, 1408), "B": (1408, 2816), "Z": (2816, 4096)}
NEAR, MID, FAR = (1, 3, 4), (2, 7, 5), 6
SLOTS = (0,) + NEAR + MID + (FAR,)


def over(array, dim):
    return lax.ppermute(array, "head", [(i, i ^ MASK[dim]) for i in range(8)])


def along(array, to):
    return lax.ppermute(array, "seq", [(i, to(i)) for i in range(16)])


def position():
    seq = lax.axis_index("seq")
    return lax.axis_index("head"), seq & 1, (seq >> 1) & 1, seq >> 2


def budget(mib):
    return pltpu.CompilerParams(vmem_limit_bytes=mib << 20)


def dot(a, b):
    return jnp.dot(a, b, preferred_element_type=f32)


def vmem(count):
    return [pl.BlockSpec(memory_space=pltpu.VMEM)] * count


def smem():
    return pl.BlockSpec(memory_space=pltpu.SMEM)


def norm_kernel(hidden, masked, embed, gain, out):
    row = lax.broadcasted_iota(jnp.int32, (PIECE, 128), 0)
    flag = jnp.zeros((PIECE, 128), jnp.int32)
    for i in range(PIECE):
        flag = jnp.where(row == i, masked[i], flag)
    source = jnp.where(flag[:, 0:1] == 1, embed[...].astype(f32)[None, :], hidden[...].astype(f32))
    mean = jnp.mean(source * source, axis=1, keepdims=True)
    out[...] = (source * lax.rsqrt(mean + EPSILON) * gain[...]).astype(bf16)


def input_norm(hidden, masked, embed, gain):
    return pl.pallas_call(
        norm_kernel,
        out_shape=jax.ShapeDtypeStruct(hidden.shape, bf16),
        in_specs=[vmem(1)[0], smem()] + vmem(2),
        out_specs=vmem(1)[0],
        compiler_params=budget(6),
        name="input_norm",
    )(hidden, masked, embed, gain[None, :])


def softplus(x):
    return jnp.maximum(x, 0.0) + jnp.log1p(jnp.exp(-jnp.abs(x)))


def silu(x):
    return x / (1.0 + jnp.exp(-x))


def pair_lanes(left, right):
    lane = lax.broadcasted_iota(jnp.int32, left.shape, 1)
    return jnp.where(lane < HEAD_DIM, left, right)


def heads_column(scalars):
    row = lax.broadcasted_iota(jnp.int32, (OWN, ROWS), 0)
    out = jnp.zeros((OWN, ROWS), f32)
    for h in range(OWN):
        out = jnp.where(row == h, scalars[h], out)
    return out


def heads_row(scalars):
    lane = lax.broadcasted_iota(jnp.int32, (1, WIDE), 1)
    out = jnp.zeros((1, WIDE), f32)
    for h in range(OWN):
        out = jnp.where(lane >= h * HEAD_DIM, scalars[h], out)
    return out


def spread(column):
    parts = []
    for q in range(OWN // 2):
        a = jnp.broadcast_to(column[2 * q : 2 * q + 1, :], (1, 128))
        b = jnp.broadcast_to(column[2 * q + 1 : 2 * q + 2, :], (1, 128))
        parts.append(pair_lanes(a, b))
    return jnp.concatenate(parts, axis=1)


def state_kernel(
    proj1, proj2, proj3, bias_f, bias_r, rate_f, rate_r,
    pay, values, b_out, c_out, rows_out, cols_out, start_f, start_r, decay_out,
    step_scratch, v3, b3, c3,
):
    me = position()[0]
    places = [(proj1, 0), (proj1, 64), (proj1, 128), (proj1, 192), (proj2, 0), (proj2, 64), (proj2, 128), (proj3, 0)]
    for mask, (ref, row) in zip(SLOTS, places, strict=True):
        at = me ^ mask
        v3[at] = silu(ref[row : row + PIECE, 0:WIDE]).astype(bf16)
        b3[at] = ref[row : row + PIECE, WIDE : WIDE + STATE]
        c3[at] = ref[row : row + PIECE, WIDE + STATE : WIDE + 2 * STATE].astype(bf16)
        step_scratch[at] = ref[row : row + PIECE, WIDE + 2 * STATE : WIDE + 3 * STATE]
    values[...] = v3[...].reshape(ROWS, WIDE)
    b_all = b3[...].reshape(ROWS, STATE).astype(bf16)
    b_out[...] = b_all
    c_out[...] = c3[...].reshape(ROWS, STATE)
    steps = step_scratch[...].reshape(ROWS, STATE).T[0:OWN, :]
    dt_f = softplus(steps + heads_column(bias_f))
    dt_r = softplus(steps + heads_column(bias_r))
    cum_f = -heads_column(rate_f) * dt_f
    cum_r = -heads_column(rate_r) * dt_r
    lane = lax.broadcasted_iota(jnp.int32, (OWN, ROWS), 1)
    inner = lane & (BLOCK - 1)
    k = 1
    while k < BLOCK:
        cum_f = cum_f + jnp.where(inner >= k, pltpu.roll(cum_f, k, 1), 0.0)
        cum_r = cum_r + jnp.where(inner < BLOCK - k, pltpu.roll(cum_r, ROWS - k, 1), 0.0)
        k *= 2
    rows = jnp.concatenate([cum_f, cum_r, dt_f, dt_r], axis=0)
    rows_out[...] = rows
    padded = jnp.concatenate([rows, jnp.zeros((STATE - 4 * OWN, ROWS), f32)], axis=0)
    cols_out[...] = padded.T
    tot_f = [cum_f[:, BLOCK - 1 : BLOCK], cum_f[:, ROWS - 1 : ROWS]]
    tot_r = [cum_r[:, 0:1], cum_r[:, BLOCK : BLOCK + 1]]
    first = lane < BLOCK
    end_f = jnp.exp(jnp.where(first, tot_f[0], tot_f[1]) - cum_f) * dt_f
    end_r = jnp.exp(jnp.where(first, tot_r[0], tot_r[1]) - cum_r) * dt_r
    states = []
    for block in range(2):
        span = slice(block * BLOCK, (block + 1) * BLOCK)
        b_t = b_all[span, :].astype(f32).T
        parts_f, parts_r = [], []
        for q in range(OWN // 2):
            lhs = jnp.concatenate(
                [(b_t * end[h : h + 1, span]).astype(bf16) for h in (2 * q, 2 * q + 1) for end in (end_f, end_r)],
                axis=0,
            )
            out = dot(lhs, values[span, q * 128 : (q + 1) * 128])
            parts_f.append(pair_lanes(out[0:128], out[256:384]))
            parts_r.append(pair_lanes(out[128:256], out[384:512]))
        states.append((jnp.concatenate(parts_f, axis=1), jnp.concatenate(parts_r, axis=1)))
    d_f = [spread(jnp.exp(t)) for t in tot_f]
    d_r = [spread(jnp.exp(t)) for t in tot_r]
    start_f[...] = states[0][0]
    start_r[...] = states[1][1]
    decay_out[0:1, :] = d_f[0]
    decay_out[1:2, :] = d_r[1]
    decay_out[2:8, :] = jnp.zeros((6, WIDE), f32)
    pay[0:STATE, :] = (d_f[1] * states[0][0] + states[1][0]).astype(bf16)
    pay[PAY : PAY + STATE, :] = (d_r[0] * states[1][1] + states[0][1]).astype(bf16)
    row = lax.broadcasted_iota(jnp.int32, (8, WIDE), 0)
    for at, total in ((STATE, d_f[0] * d_f[1]), (PAY + STATE, d_r[0] * d_r[1])):
        high = total.astype(bf16).astype(f32)
        tail = jnp.where(row == 0, high, jnp.where(row == 1, total - high, 0.0))
        pay[at : at + 8, :] = tail.astype(bf16)


def piece_states(proj1, proj2, proj3, bias_f, bias_r, rate_f, rate_r):
    shapes = [
        ((2 * PAY, WIDE), bf16),
        ((ROWS, WIDE), bf16),
        ((ROWS, STATE), bf16),
        ((ROWS, STATE), bf16),
        ((4 * OWN, ROWS), f32),
        ((ROWS, STATE), f32),
        ((STATE, WIDE), f32),
        ((STATE, WIDE), f32),
        ((8, WIDE), f32),
    ]
    return pl.pallas_call(
        state_kernel,
        out_shape=[jax.ShapeDtypeStruct(s, d) for s, d in shapes],
        in_specs=vmem(3) + [smem()] * 4,
        out_specs=vmem(9),
        scratch_shapes=[
            pltpu.VMEM((8, PIECE, STATE), f32),
            pltpu.VMEM((8, PIECE, WIDE), bf16),
            pltpu.VMEM((8, PIECE, STATE), f32),
            pltpu.VMEM((8, PIECE, STATE), bf16),
        ],
        compiler_params=budget(14),
        name="piece_states",
    )(proj1, proj2, proj3, bias_f, bias_r, rate_f, rate_r)


def inside_kernel(
    block, gate1, gate2, gate3, values, b_rows, c_rows, rows, cols, skip_f, skip_r,
    base_f, base_r, factor_f, factor_r, g3,
):
    me = position()[0]
    places = [(gate1, 0), (gate1, 64), (gate1, 128), (gate1, 192), (gate2, 0), (gate2, 64), (gate2, 128), (gate3, 0)]
    for mask, (ref, row) in zip(SLOTS, places, strict=True):
        at = (me ^ mask) - 4 * block

        @pl.when((at >= 0) & (at < 4))
        def _(ref=ref, row=row, at=at):
            g3[at] = silu(ref[row : row + PIECE, :])

    below = lax.broadcasted_iota(jnp.int32, (128, 128), 0) >= lax.broadcasted_iota(jnp.int32, (128, 128), 1)
    above = lax.broadcasted_iota(jnp.int32, (128, 128), 0) <= lax.broadcasted_iota(jnp.int32, (128, 128), 1)
    nothing = jnp.zeros((128, 128), bf16)
    skips = heads_row(skip_f), heads_row(skip_r)
    lo = block * BLOCK
    span = slice(lo, lo + BLOCK)
    scores = lax.dot_general(
        c_rows[span, :], b_rows[span, :], (((1,), (1,)), ((), ())), preferred_element_type=f32
    )
    gate = g3[...].reshape(BLOCK, WIDE)
    for q in range(OWN // 2):
        lhs, grow = [], []
        for h in (2 * q, 2 * q + 1):
            for way in range(2):
                at = way * OWN + h
                col = jnp.broadcast_to(cols[span, at : at + 1], (BLOCK, 128))
                grow.append(jnp.exp(col))
                tiles = {}
                for t, s in (((0, 0), (1, 0), (1, 1)), ((0, 0), (0, 1), (1, 1)))[way]:
                    cut = slice(lo + s * 128, lo + (s + 1) * 128)
                    differ = col[t * 128 : (t + 1) * 128] - rows[at : at + 1, cut]
                    if t == s:
                        differ = jnp.where(above if way else below, differ, -1e30)
                    weight = jnp.exp(differ) * rows[2 * OWN + at : 2 * OWN + at + 1, cut]
                    tiles[t, s] = (scores[t * 128 : (t + 1) * 128, s * 128 : (s + 1) * 128] * weight).astype(bf16)
                for t in range(2):
                    lhs.append(jnp.concatenate([tiles.get((t, s), nothing) for s in range(2)], axis=1))
        wide = slice(q * 128, (q + 1) * 128)
        value = values[span, wide]
        out = dot(jnp.concatenate(lhs, axis=0), value)
        value = value.astype(f32)
        g = gate[:, wide]
        for way, (base, factor) in enumerate(((base_f, factor_f), (base_r, factor_r))):
            a, b = way * BLOCK, (2 + way) * BLOCK
            inside = pair_lanes(out[a : a + BLOCK], out[b : b + BLOCK])
            base[:, wide] = (inside + skips[way][:, wide] * value) * g
            factor[:, wide] = pair_lanes(grow[way], grow[2 + way]) * g


def inside_block(block, gate1, gate2, gate3, values, b_rows, c_rows, rows, cols, skip_f, skip_r):
    return pl.pallas_call(
        functools.partial(inside_kernel, block),
        out_shape=[jax.ShapeDtypeStruct((BLOCK, WIDE), f32)] * 4,
        in_specs=vmem(8) + [smem()] * 2,
        out_specs=vmem(4),
        scratch_shapes=[pltpu.VMEM((4, PIECE, WIDE), f32)],
        compiler_params=budget(14),
    )(gate1, gate2, gate3, values, b_rows, c_rows, rows, cols, skip_f, skip_r)


HALF = WIDE // 2


def read_pay(ref, at, lanes=slice(None)):
    tail = ref[at + STATE : at + PAY, lanes].astype(f32)
    return ref[at : at + STATE, lanes].astype(f32), tail[0:1] + tail[1:2]


def write_pay(ref, at, state, decay):
    ref[at : at + STATE, :] = state.astype(bf16)
    row = lax.broadcasted_iota(jnp.int32, (PAY - STATE, state.shape[1]), 0)
    high = decay.astype(bf16).astype(f32)
    tail = jnp.where(row == 0, high, jnp.where(row == 1, decay - high, 0.0))
    ref[at + STATE : at + PAY, :] = tail.astype(bf16)


def choose(cond, a, b):
    return jnp.where(cond, a[0], b[0]), jnp.where(cond, a[1], b[1])


def joined(mine, his, mine_later):
    first, second = choose(mine_later, his, mine), choose(mine_later, mine, his)
    return second[1] * first[0] + second[0], first[1] * second[1]


def chip_kernel(pay, other, out):
    core = position()[1]
    left, right = slice(0, HALF), slice(HALF, WIDE)
    for way, at in enumerate((0, PAY)):
        mine, his = [choose(core == 0, read_pay(p, at, left), read_pay(p, at, right)) for p in (pay, other)]
        write_pay(out, at, *joined(mine, his, core == 1 - way))


def pair_kernel(chip, beside, *outs):
    _, _, z, x = position()
    total = [joined(read_pay(chip, at), read_pay(beside, at), z == 1 - way) for way, at in enumerate((0, PAY))]
    for k, out in enumerate(outs, start=1):
        write_pay(out, 0, *choose(x + k < 4, *total))


def enter_kernel(got1, got2, got3, beside, out):
    _, _, z, x = position()
    got = [read_pay(g, 0) for g in (got1, got2, got3)]
    keep = lambda c, a: jnp.where(c, a, 0.0)
    for way in range(2):
        near, mid, far = got if way == 0 else got[::-1]
        step = x if way == 0 else 3 - x
        enter = keep(step >= 1, near[0])
        enter += keep(step >= 2, near[1] * mid[0])
        enter += keep(step >= 3, near[1] * mid[1] * far[0])
        state, decay = read_pay(beside, way * PAY)
        enter = jnp.where(z == 1 - way, decay * enter + state, enter)
        out[way * STATE : (way + 1) * STATE, :] = enter.astype(bf16)


def small_call(kernel, shapes, *arrays):
    return pl.pallas_call(
        kernel,
        out_shape=[jax.ShapeDtypeStruct(s, bf16) for s in shapes],
        in_specs=vmem(len(arrays)),
        out_specs=vmem(len(shapes)),
        compiler_params=budget(6),
    )(*arrays)


def entering_states(pay):
    other = along(pay, lambda i: i ^ 1)
    (chip,) = small_call(chip_kernel, [(2 * PAY, HALF)], pay, other)
    beside = along(chip, lambda i: i ^ 2)
    sent = small_call(pair_kernel, [(PAY, HALF)] * 3, chip, beside)
    got = []
    for k in (1, 2, 3):
        got.append(lax.ppermute(sent[k - 1], "seq", [(i, (i + 4 * k) % 16) for i in range(16)]))
    (mine,) = small_call(enter_kernel, [(2 * STATE, HALF)], *got, beside)
    return mine, along(mine, lambda i: i ^ 1), other


def gated_kernel(
    mine, his, other, start_f, start_r, decay, c_rows, inside0, inside1, gain,
    out_f, out_r, far, square, gated3,
):
    me, core, _, _ = position()
    a, b = mine[...].astype(f32), his[...].astype(f32)
    zero = core == 0
    enter = jnp.concatenate([jnp.where(zero, a, b), jnp.where(zero, b, a)], axis=1)
    enter_f, enter_r = enter[:STATE], enter[STATE:]
    state, fade = read_pay(other, 0)
    enter_f = jnp.where(zero, enter_f, fade * enter_f + state)
    state, fade = read_pay(other, PAY)
    enter_r = jnp.where(zero, fade * enter_r + state, enter_r)
    at_f = (enter_f, decay[0:1, :] * enter_f + start_f[...])
    at_r = (decay[1:2, :] * enter_r + start_r[...], enter_r)
    ones = jnp.ones((8, WIDE), bf16)
    pick = lax.broadcasted_iota(jnp.int32, (8, BLOCK), 0)
    for block in range(2):
        span = slice(block * BLOCK, (block + 1) * BLOCK)
        c_blk = c_rows[span, :]
        base_f, base_r, factor_f, factor_r = (inside0, inside1)[block]
        sums = []
        for way, (at, base, factor) in enumerate(((at_f, base_f, factor_f), (at_r, base_r, factor_r))):
            gated = base[...] + dot(c_blk, at[block].astype(bf16)) * factor[...]
            sums.append(
                lax.dot_general(ones, (gated * gated).astype(bf16), (((1,), (1,)), ((), ())), preferred_element_type=f32)
            )
            gated3[way, 4 * block : 4 * block + 4] = (gated * gain[...]).reshape(4, PIECE, WIDE)
        square[:, span] = jnp.where(pick == 0, sums[0], sums[1])
    for slot, mask in enumerate(SLOTS):
        at = me ^ mask
        out_f[slot] = gated3[0, at]
        out_r[slot] = gated3[1, at]
    far[0:PIECE, :] = out_f[7].astype(bf16)
    far[PIECE : 2 * PIECE, :] = out_r[7].astype(bf16)


def gated_outputs(mine, his, other, start_f, start_r, decay, c_rows, inside0, inside1, gain):
    def kernel(a, b, c, d, e, f, g, *refs):
        gated_kernel(a, b, c, d, e, f, g, refs[0:4], refs[4:8], *refs[8:])

    return pl.pallas_call(
        kernel,
        out_shape=[
            jax.ShapeDtypeStruct((8, PIECE, WIDE), f32),
            jax.ShapeDtypeStruct((8, PIECE, WIDE), f32),
            jax.ShapeDtypeStruct((2 * PIECE, WIDE), bf16),
            jax.ShapeDtypeStruct((8, ROWS), f32),
        ],
        in_specs=vmem(16),
        out_specs=vmem(4),
        scratch_shapes=[pltpu.VMEM((2, 8, PIECE, WIDE), f32)],
        compiler_params=budget(16),
        name="gated_outputs",
    )(mine, his, other, start_f, start_r, decay, c_rows, *inside0, *inside1, gain)


def scale_kernel(gated_f, gated_r, square, *refs):
    outs, scale_out, scale3 = refs[:-2], refs[-2], refs[-1]
    me = position()[0]
    scale = lax.rsqrt(square[...] / float(HEADS * HEAD_DIM) + EPSILON)
    padded = jnp.concatenate([scale, jnp.zeros((120, ROWS), f32)], axis=0)
    scale3[...] = padded.T.reshape(8, PIECE, 128)
    slot = 0
    for out in outs:
        for i in range(out.shape[0] // PIECE):
            here = scale3[me ^ SLOTS[slot]]
            scale_out[slot] = here
            out[i * PIECE : (i + 1) * PIECE, :] = (
                gated_f[slot] * here[:, 0:1] + gated_r[slot] * here[:, 1:2]
            ).astype(bf16)
            slot += 1


def scaled_outputs(gated_f, gated_r, square):
    return pl.pallas_call(
        scale_kernel,
        out_shape=[jax.ShapeDtypeStruct((n * PIECE, WIDE), bf16) for n in (1, 3, 3)]
        + [jax.ShapeDtypeStruct((7, PIECE, 128), f32)],
        in_specs=vmem(3),
        out_specs=vmem(4),
        scratch_shapes=[pltpu.VMEM((8, PIECE, 128), f32)],
        compiler_params=budget(10),
        name="scaled_outputs",
    )(gated_f, gated_r, square)


def on_device(
    hidden,
    masked,
    mask_embed,
    in_gain,
    w_gate,
    w_value,
    w_step,
    w_bc,
    dt_bias_forward,
    dt_bias_reverse,
    rate_forward,
    rate_reverse,
    skip_forward,
    skip_reverse,
    out_gain,
    w_out,
):
    own = input_norm(hidden, masked, mask_embed, in_gain)

    def send(dim, array):
        return over(array, dim)

    at_a, at_b, at_z = [send(dim, own) for dim in "ABZ"]
    at_za = send("Z", at_a)
    at_bz = send("B", at_z)
    at_ab = send("A", at_b)
    part = lambda array, dim: array[:, slice(*CUT[dim])]
    far = [send(dim, part(array, dim)) for dim, array in (("A", at_bz), ("B", at_za), ("Z", at_ab))]
    weights = jnp.concatenate([w_value, w_bc, jnp.pad(w_step, ((0, 0), (0, STATE - OWN)))], axis=1)
    proj, gate = [], []
    for i, blocks in enumerate(((own, at_a, at_b, at_z), (at_ab, at_bz, at_za), far), start=1):
        stage = jnp.concatenate(blocks, axis=0 if i < 3 else 1)
        proj.append(dot(stage, weights))
        gate.append(dot(stage, w_gate))

    pay, values, b_rows, c_rows, rows, cols, start_f, start_r, decay = piece_states(
        *proj, dt_bias_forward, dt_bias_reverse, rate_forward, rate_reverse
    )
    mine, his, other = entering_states(pay)
    inside = []
    for block in range(2):
        inside.append(
            inside_block(block, *gate, values, b_rows, c_rows, rows, cols, skip_forward, skip_reverse)
        )
    gated_f, gated_r, far, square = gated_outputs(
        mine, his, other, start_f, start_r, decay, c_rows, *inside, out_gain[None, :]
    )
    p_far = dot(far, w_out).astype(bf16)
    got = {dim: send(dim, part(p_far, dim)) for dim in "ABZ"}
    for dim in "ABZ":
        square = square + send(dim, square)
    n_own, n_near, n_mid, scale = scaled_outputs(gated_f, gated_r, square)
    p_mid = dot(n_mid, w_out)

    def with_part(mask, dim):
        i = MID.index(mask)
        piece, here = p_mid[i * PIECE : (i + 1) * PIECE], scale[4 + i]
        a, b = CUT[dim]
        arrived = got[dim].astype(f32)
        arrived = arrived[:PIECE] * here[:, 0:1] + arrived[PIECE:] * here[:, 1:2]
        return jnp.concatenate([piece[:, :a], piece[:, a:b] + arrived, piece[:, b:]], axis=1).astype(bf16)

    got_b = send("A", with_part(2, "Z"))
    got_z = send("B", with_part(7, "A"))
    got_a = send("Z", with_part(5, "B"))
    p_near = dot(n_near, w_out)
    p_near = lax.optimization_barrier([p_near[i * PIECE : (i + 1) * PIECE] for i in range(3)])
    total = dot(n_own, w_out)
    near = lambda i, arrived: (p_near[i] + arrived.astype(f32)).astype(bf16)
    last = [send("A", near(0, got_a)), send("B", near(1, got_b)), send("Z", near(2, got_z))]
    for arrived in last:
        total = total + arrived.astype(f32)
    return total.astype(bf16)


def solution(mesh):
    in_specs = (
        P(("seq", "head"), None),
        P(("seq", "head")),
        P(),
        P(),
        P(None, "head"),
        P(None, "head"),
        P(None, "head"),
        P(),
        P("head"),
        P("head"),
        P("head"),
        P("head"),
        P("head"),
        P("head"),
        P("head"),
        P("head", None),
    )
    out_specs = P(("seq", "head"), None)
    return jax.shard_map(on_device, mesh=mesh, in_specs=in_specs, out_specs=out_specs, check_vma=False)
```

profile of v0, /device:TPU:1, one launch (start us, length us, event | category | flops | bytes accessed | tf_op | source)
XLA Modules:
  0.0 117.2 jit_solution(4195848570207083768)
XLA Ops:
  4.0 2.5 %collective-permute-start.2 = (bf16[64,4096]{1,0:T(8,128)(2,1)S(1)}, bf16[64,4096]{1,0:T(8,128)(2,1)S(1)}, u32[]{:S(2)}, u32[]{:S(2)}) collective-permute-start(bf16[64,4096]{1,0:T(8,128)(2,1)S(1)} %input_norm.1), channel_id=1, source_target_pairs={{0,4},{1,5},{2,6},{3,7},{4,0},{5,1},{6,2},{7,3},{8,12},{9,13},{10,... | collective-permute-start | bytes 1572872 | tf_op jit(solution)/shard_map/ppermute | solution.py:32
  6.6 2.7 %collective-permute-start.1 = (bf16[64,4096]{1,0:T(8,128)(2,1)S(1)}, bf16[64,4096]{1,0:T(8,128)(2,1)S(1)}, u32[]{:S(2)}, u32[]{:S(2)}) collective-permute-start(bf16[64,4096]{1,0:T(8,128)(2,1)S(1)} %input_norm.1), channel_id=1, source_target_pairs={{0,3},{1,2},{2,1},{3,0},{4,7},{5,6},{6,5},{7,4},{8,11},{9,10},{10,... | collective-permute-start | bytes 1572872 | tf_op jit(solution)/shard_map/ppermute | solution.py:32
  9.3 1.3 %copy.19 = bf16[4096,8]{1,0:T(8,128)(2,1)S(1)} copy(bf16[4096,8]{0,1:T(8,128)(2,1)} %param.22) | data formatting | bytes 131072
  10.6 3.7 %fusion.1 = bf16[4096,896]{1,0:T(8,128)(2,1)S(1)} fusion(bf16[4096,8]{1,0:T(8,128)(2,1)S(1)} %copy.19, bf16[4096,256]{1,0:T(8,128)(2,1)} %param.23, bf16[4096,512]{1,0:T(8,128)(2,1)} %param.21), kind=kLoop, calls=%fused_computation.2 | loop fusion | flops 29360128 | bytes 13697024 | tf_op jit(solution)/shard_map/concatenate | solution.py:471
  14.3 3.9 %collective-permute-done.2 = bf16[64,4096]{1,0:T(8,128)(2,1)S(1)} collective-permute-done((bf16[64,4096]{1,0:T(8,128)(2,1)S(1)}, bf16[64,4096]{1,0:T(8,128)(2,1)S(1)}, u32[]{:S(2)}, u32[]{:S(2)}) %collective-permute-start.2) | collective-permute-done | bytes 524320 | tf_op jit(solution)/shard_map/ppermute | solution.py:32
  18.2 2.6 %collective-permute-start.4 = (bf16[64,4096]{1,0:T(8,128)(2,1)S(1)}, bf16[64,4096]{1,0:T(8,128)(2,1)S(1)}, u32[]{:S(2)}, u32[]{:S(2)}) collective-permute-start(bf16[64,4096]{1,0:T(8,128)(2,1)S(1)} %collective-permute-done.2), channel_id=1, source_target_pairs={{0,3},{1,2},{2,1},{3,0},{4,7},{5,6},{6,5},{7,4},{8,11},{9,10},{10,... | collective-permute-start | bytes 1572872 | tf_op jit(solution)/shard_map/ppermute | solution.py:32
  22.2 2.3 %fusion.12.proj1 = f32[256,896]{1,0:T(8,128)S(1)} fusion(bf16[4096,896]{1,0:T(8,128)(2,1)S(1)} %fusion.1, bf16[64,4096]{1,0:T(8,128)(2,1)S(1)} %collective-permute-done.2, bf16[64,4096]{1,0:T(8,128)(2,1)S(1)} %collective-permute-done.1, bf16[64,4096]{1,0:T(8,128)(2,1)S(1)} %collective-permute-done, bf16[64,4096]{1,0:T(8,128)(2,1)S(1)} %input_norm.1), kind=kOutput, calls=%fused_computation.26 | convolution fusion | flops 1887436800 | bytes 10354688 | tf_op jit(solution)/shard_map/dot_general | solution.py:49
  24.5 7.1 %collective-permute-done.4 = bf16[64,4096]{1,0:T(8,128)(2,1)S(1)} collective-permute-done((bf16[64,4096]{1,0:T(8,128)(2,1)S(1)}, bf16[64,4096]{1,0:T(8,128)(2,1)S(1)}, u32[]{:S(2)}, u32[]{:S(2)}) %collective-permute-start.4) | collective-permute-done | bytes 524320 | tf_op jit(solution)/shard_map/ppermute | solution.py:32
  33.9 1.7 %collective-permute-start.7 = (bf16[64,1408]{1,0:T(8,128)(2,1)S(1)}, bf16[64,1408]{1,0:T(8,128)(2,1)S(1)}, u32[]{:S(2)}, u32[]{:S(2)}) collective-permute-start(bf16[64,1408]{1,0:T(8,128)(2,1)S(1)} %slice.139), channel_id=1, source_target_pairs={{0,3},{1,2},{2,1},{3,0},{4,7},{5,6},{6,5},{7,4},{8,11},{9,10},{10,... | collective-permute-start | bytes 540680 | tf_op jit(solution)/shard_map/ppermute | solution.py:32
  35.7 1.8 %fusion.21.proj2 = f32[192,896]{1,0:T(8,128)S(1)} fusion(bf16[192,4096]{1,0:T(8,128)(2,1)S(1)} %constant_dynamic-update-slice_fusion, bf16[4096,896]{1,0:T(8,128)(2,1)S(1)} %fusion.1), kind=kOutput, calls=%fused_computation.52 | convolution fusion | flops 1409286144 | bytes 9601024 | tf_op jit(solution)/shard_map/dot_general | solution.py:49
  37.6 1.9 %collective-permute-done.7 = bf16[64,1408]{1,0:T(8,128)(2,1)S(1)} collective-permute-done((bf16[64,1408]{1,0:T(8,128)(2,1)S(1)}, bf16[64,1408]{1,0:T(8,128)(2,1)S(1)}, u32[]{:S(2)}, u32[]{:S(2)}) %collective-permute-start.7) | collective-permute-done | bytes 180256 | tf_op jit(solution)/shard_map/ppermute | solution.py:32
  39.6 1.3 %fusion.22.proj3 = f32[64,896]{1,0:T(8,128)S(1)} fusion(bf16[64,4096]{1,0:T(8,128)(2,1)S(1)} %constant_dynamic-update-slice_fusion.3, bf16[4096,896]{1,0:T(8,128)(2,1)S(1)} %fusion.1), kind=kOutput, calls=%fused_computation.53 | convolution fusion | flops 469762048 | bytes 8093696 | tf_op jit(solution)/shard_map/dot_general | solution.py:49
  40.9 2.3 %piece_states.1 = (bf16[272,512]{1,0:T(8,128)(2,1)S(1)}, bf16[512,512]{1,0:T(8,128)(2,1)S(1)}, bf16[512,128]{1,0:T(8,128)(2,1)S(1)}, bf16[512,128]{1,0:T(8,128)(...) custom-call(f32[256,896]{1,0:T(8,128)S(1)} %fusion.12.proj1, ...), custom_call_target="tpu_custom_call" | custom-call | tf_op jit(solution)/shard_map/piece_states/pallas_call | solution.py:199
  43.2 4.8 %collective-permute-start.9 = (bf16[272,512]{1,0:T(8,128)(2,1)S(1)}, bf16[272,512]{1,0:T(8,128)(2,1)S(1)}, u32[]{:S(2)}, u32[]{:S(2)}) collective-permute-start(bf16[272,512]{1,0:T(8,128)(2,1)S(1)} %get-tuple-element.36.pay), channel_id=1, source_target_pairs={{0,8},{8,0},{16,24},{24,16},{32,40},{40,32},{48,56},{56,48},{64,72... | collective-permute-start | bytes 835592 | tf_op jit(solution)/shard_map/ppermute | solution.py:36
  49.3 3.4 %collective-permute-start.10 = (bf16[272,256]{1,0:T(8,128)(2,1)S(1)}, bf16[272,256]{1,0:T(8,128)(2,1)S(1)}, u32[]{:S(2)}, u32[]{:S(2)}) collective-permute-start(bf16[272,256]{1,0:T(8,128)(2,1)S(1)} %shard_map.154.chip), channel_id=1, source_target_pairs={{0,16},{8,24},{16,0},{24,8},{32,48},{40,56},{48,32},{56,40},{64,80... | collective-permute-start | bytes 417800 | tf_op jit(solution)/shard_map/ppermute | solution.py:36
  53.9 2.4 %collective-permute-done.10.beside = bf16[272,256]{1,0:T(8,128)(2,1)S(1)} collective-permute-done((bf16[272,256]{1,0:T(8,128)(2,1)S(1)}, bf16[272,256]{1,0:T(8,128)(2,1)S(1)}, u32[]{:S(2)}, u32[]{:S(2)}) %collective-permute-start.10) | collective-permute-done | bytes 139296 | tf_op jit(solution)/shard_map/ppermute | solution.py:36
  56.4 1.3 %collective-permute-start.11 = (bf16[136,256]{1,0:T(8,128)(2,1)S(1)}, bf16[136,256]{1,0:T(8,128)(2,1)S(1)}, u32[]{:S(2)}, u32[]{:S(2)}) collective-permute-start(bf16[136,256]{1,0:T(8,128)(2,1)S(1)} %get-tuple-element.37), channel_id=1, source_target_pairs={{0,32},{8,40},{16,48},{24,56},{32,64},{40,72},{48,80},{56,88},{64,... | collective-permute-start | bytes 208904 | tf_op jit(solution)/shard_map/ppermute | solution.py:350
  57.7 2.4 %collective-permute-start.12 = (bf16[136,256]{1,0:T(8,128)(2,1)S(1)}, bf16[136,256]{1,0:T(8,128)(2,1)S(1)}, u32[]{:S(2)}, u32[]{:S(2)}) collective-permute-start(bf16[136,256]{1,0:T(8,128)(2,1)S(1)} %get-tuple-element.38), channel_id=1, source_target_pairs={{0,64},{8,72},{16,80},{24,88},{32,96},{40,104},{48,112},{56,120},{... | collective-permute-start | bytes 208904 | tf_op jit(solution)/shard_map/ppermute | solution.py:350
  62.7 1.5 %collective-permute-done.13.got3 = bf16[136,256]{1,0:T(8,128)(2,1)S(1)} collective-permute-done((bf16[136,256]{1,0:T(8,128)(2,1)S(1)}, bf16[136,256]{1,0:T(8,128)(2,1)S(1)}, u32[]{:S(2)}, u32[]{:S(2)}) %collective-permute-start.13) | collective-permute-done | bytes 69664 | tf_op jit(solution)/shard_map/ppermute | solution.py:350
  64.3 1.9 %collective-permute-start.14 = (bf16[256,256]{1,0:T(8,128)(2,1)S(1)}, bf16[256,256]{1,0:T(8,128)(2,1)S(1)}, u32[]{:S(2)}, u32[]{:S(2)}) collective-permute-start(bf16[256,256]{1,0:T(8,128)(2,1)S(1)} %shard_map.156.a), channel_id=1, source_target_pairs={{0,8},{8,0},{16,24},{24,16},{32,40},{40,32},{48,56},{56,48},{64,72... | collective-permute-start | bytes 393224 | tf_op jit(solution)/shard_map/ppermute | solution.py:36
  67.1 2.2 %shard_map.158 = (f32[256,512]{1,0:T(8,128)S(1)}, f32[256,512]{1,0:T(8,128)S(1)}, f32[256,512]{1,0:T(8,128)S(1)}, f32[256,512]{1,0:T(8,128)S(1)}) custom-call(f32[256,512]{1,0:T(8,128)S(1)} %fusion.11.gate1, f32[192,512]{1,0:T(8,128)S(1)} %fusion.23.gate2, f32[64,512]{1,0:T(8,128)S(1)} %fusion.24.gate3, bf16[512,512]{1,0:T(8,128)(2,1)S(1)} %get-tuple-element.44.values, ...), custom_call_target="tpu_custom_call" | custom-call | tf_op jit(solution)/shard_map/pallas_call | solution.py:268
  69.3 2.2 %shard_map.157 = (f32[256,512]{1,0:T(8,128)S(1)}, f32[256,512]{1,0:T(8,128)S(1)}, f32[256,512]{1,0:T(8,128)S(1)}, f32[256,512]{1,0:T(8,128)S(1)}) custom-call(f32[256,512]{1,0:T(8,128)S(1)} %fusion.11.gate1, f32[192,512]{1,0:T(8,128)S(1)} %fusion.23.gate2, f32[64,512]{1,0:T(8,128)S(1)} %fusion.24.gate3, bf16[512,512]{1,0:T(8,128)(2,1)S(1)} %get-tuple-element.44.values, ...), custom_call_target="tpu_custom_call" | custom-call | tf_op jit(solution)/shard_map/pallas_call | solution.py:268
  72.6 2.6 %collective-permute-done.15 = f32[8,512]{1,0:T(8,128)S(1)} collective-permute-done((f32[8,512]{1,0:T(8,128)S(1)}, f32[8,512]{1,0:T(8,128)S(1)}, u32[]{:S(2)}, u32[]{:S(2)}) %collective-permute-start.15) | collective-permute-done | bytes 16416 | tf_op jit(solution)/shard_map/ppermute | solution.py:32
  76.6 2.3 %collective-permute-done.16 = f32[8,512]{1,0:T(8,128)S(1)} collective-permute-done((f32[8,512]{1,0:T(8,128)S(1)}, f32[8,512]{1,0:T(8,128)S(1)}, u32[]{:S(2)}, u32[]{:S(2)}) %collective-permute-start.16) | collective-permute-done | bytes 16416 | tf_op jit(solution)/shard_map/ppermute | solution.py:32
  79.1 1.5 %collective-permute-start.21 = (bf16[128,1280]{1,0:T(8,128)(2,1)S(1)}, bf16[128,1280]{1,0:T(8,128)(2,1)S(1)}, u32[]{:S(2)}, u32[]{:S(2)}) collective-permute-start(bf16[128,1280]{1,0:T(8,128)(2,1)S(1)} %slice.154), channel_id=1, source_target_pairs={{0,4},{1,5},{2,6},{3,7},{4,0},{5,1},{6,2},{7,3},{8,12},{9,13},{10,... | collective-permute-start | bytes 983048 | tf_op jit(solution)/shard_map/ppermute | solution.py:32
  84.9 1.4 %collective-permute-done.21 = bf16[128,1280]{1,0:T(8,128)(2,1)S(1)} collective-permute-done((bf16[128,1280]{1,0:T(8,128)(2,1)S(1)}, bf16[128,1280]{1,0:T(8,128)(2,1)S(1)}, u32[]{:S(2)}, u32[]{:S(2)}) %collective-permute-start.21) | collective-permute-done | bytes 327712 | tf_op jit(solution)/shard_map/ppermute | solution.py:32
  86.6 2.3 %collective-permute-done.18 = bf16[128,1408]{1,0:T(8,128)(2,1)S(1)} collective-permute-done((bf16[128,1408]{1,0:T(8,128)(2,1)S(1)}, bf16[128,1408]{1,0:T(8,128)(2,1)S(1)}, u32[]{:S(2)}, u32[]{:S(2)}) %collective-permute-start.18) | collective-permute-done | bytes 360480 | tf_op jit(solution)/shard_map/ppermute | solution.py:32
  91.0 9.5 %collective-permute-done.22 = bf16[64,4096]{1,0:T(8,128)(2,1)S(1)} collective-permute-done((bf16[64,4096]{1,0:T(8,128)(2,1)S(1)}, bf16[64,4096]{1,0:T(8,128)(2,1)S(1)}, u32[]{:S(2)}, u32[]{:S(2)}) %collective-permute-start.22) | collective-permute-done | bytes 524320 | tf_op jit(solution)/shard_map/ppermute | solution.py:32
  100.7 1.5 %collective-permute-start.23 = (bf16[64,4096]{1,0:T(8,128)(2,1)S(1)}, bf16[64,4096]{1,0:T(8,128)(2,1)S(1)}, u32[]{:S(2)}, u32[]{:S(2)}) collective-permute-start(bf16[64,4096]{1,0:T(8,128)(2,1)S(1)} %add_convert_fusion.1), channel_id=1, source_target_pairs={{0,3},{1,2},{2,1},{3,0},{4,7},{5,6},{6,5},{7,4},{8,11},{9,10},{10,... | collective-permute-start | bytes 1572872 | tf_op jit(solution)/shard_map/ppermute | solution.py:32
  103.3 10.1 %collective-permute-done.23 = bf16[64,4096]{1,0:T(8,128)(2,1)S(1)} collective-permute-done((bf16[64,4096]{1,0:T(8,128)(2,1)S(1)}, bf16[64,4096]{1,0:T(8,128)(2,1)S(1)}, u32[]{:S(2)}, u32[]{:S(2)}) %collective-permute-start.23) | collective-permute-done | bytes 524320 | tf_op jit(solution)/shard_map/ppermute | solution.py:32
  113.4 1.9 %collective-permute-done.26 = bf16[64,4096]{1,0:T(8,128)(2,1)S(1)} collective-permute-done((bf16[64,4096]{1,0:T(8,128)(2,1)S(1)}, bf16[64,4096]{1,0:T(8,128)(2,1)S(1)}, u32[]{:S(2)}, u32[]{:S(2)}) %collective-permute-start.26) | collective-permute-done | bytes 524320 | tf_op jit(solution)/shard_map/ppermute | solution.py:32
  115.3 1.8 %fusion.4 = bf16[64,4096]{1,0:T(8,128)(2,1)} fusion(bf16[64,512]{1,0:T(8,128)(2,1)S(1)} %get-tuple-element.59, bf16[512,4096]{1,0:T(8,128)(2,1)S(1)} %copy-done.11, bf16[64,4096]{1,0:T(8,128)(2,1)S(1)} %collective-permute-done.26, bf16[64,4096]{1,0:T(8,128)(2,1)S(1)} %collective-permute-done.23, bf16[64,4096]{1,0:T(8,128)(2,1)S(1)} %collective-permute-done.20), kind=kOutput, calls=%fused_computation.7 | convolution fusion | flops 270270464 | bytes 6356992 | tf_op jit(solution)/shard_map/dot_general | solution.py:49
  (102 shorter events, 24.3 us)
Async XLA Ops:
  4.0 14.2 %collective-permute-start.2 = (bf16[64,4096]{1,0:T(8,128)(2,1)S(1)}, bf16[64,4096]{1,0:T(8,128)(2,1)S(1)}, u32[]{:S(2)}, u32[]{:S(2)}) collective-permute-start(bf16[64,4096]{1,0:T(8,128)(2,1)S(1)} %input_norm.1), channel_id=1, source_target_pairs={{0,4},{1,5},{2,6},{3,7},{4,0},{5,1},{6,2},{7,3},{8,12},{9,13},{10,... | collective-permute-start | bytes 1572872 | tf_op jit(solution)/shard_map/ppermute | solution.py:32
  6.6 14.3 %collective-permute-start.1 = (bf16[64,4096]{1,0:T(8,128)(2,1)S(1)}, bf16[64,4096]{1,0:T(8,128)(2,1)S(1)}, u32[]{:S(2)}, u32[]{:S(2)}) collective-permute-start(bf16[64,4096]{1,0:T(8,128)(2,1)S(1)} %input_norm.1), channel_id=1, source_target_pairs={{0,3},{1,2},{2,1},{3,0},{4,7},{5,6},{6,5},{7,4},{8,11},{9,10},{10,... | collective-permute-start | bytes 1572872 | tf_op jit(solution)/shard_map/ppermute | solution.py:32
  9.3 12.2 %collective-permute-start = (bf16[64,4096]{1,0:T(8,128)(2,1)S(1)}, bf16[64,4096]{1,0:T(8,128)(2,1)S(1)}, u32[]{:S(2)}, u32[]{:S(2)}) collective-permute-start(bf16[64,4096]{1,0:T(8,128)(2,1)S(1)} %input_norm.1), channel_id=1, source_target_pairs={{0,1},{1,0},{2,3},{3,2},{4,5},{5,4},{6,7},{7,6},{8,9},{9,8},{10,11... | collective-permute-start | bytes 1572872 | tf_op jit(solution)/shard_map/ppermute | solution.py:32
  18.2 13.4 %collective-permute-start.4 = (bf16[64,4096]{1,0:T(8,128)(2,1)S(1)}, bf16[64,4096]{1,0:T(8,128)(2,1)S(1)}, u32[]{:S(2)}, u32[]{:S(2)}) collective-permute-start(bf16[64,4096]{1,0:T(8,128)(2,1)S(1)} %collective-permute-done.2), channel_id=1, source_target_pairs={{0,3},{1,2},{2,1},{3,0},{4,7},{5,6},{6,5},{7,4},{8,11},{9,10},{10,... | collective-permute-start | bytes 1572872 | tf_op jit(solution)/shard_map/ppermute | solution.py:32
  20.8 11.8 %collective-permute-start.3 = (bf16[64,4096]{1,0:T(8,128)(2,1)S(1)}, bf16[64,4096]{1,0:T(8,128)(2,1)S(1)}, u32[]{:S(2)}, u32[]{:S(2)}) collective-permute-start(bf16[64,4096]{1,0:T(8,128)(2,1)S(1)} %collective-permute-done.1), channel_id=1, source_target_pairs={{0,1},{1,0},{2,3},{3,2},{4,5},{5,4},{6,7},{7,6},{8,9},{9,8},{10,11... | collective-permute-start | bytes 1572872 | tf_op jit(solution)/shard_map/ppermute | solution.py:32
  21.5 12.3 %collective-permute-start.5 = (bf16[64,4096]{1,0:T(8,128)(2,1)S(1)}, bf16[64,4096]{1,0:T(8,128)(2,1)S(1)}, u32[]{:S(2)}, u32[]{:S(2)}) collective-permute-start(bf16[64,4096]{1,0:T(8,128)(2,1)S(1)} %collective-permute-done), channel_id=1, source_target_pairs={{0,4},{1,5},{2,6},{3,7},{4,0},{5,1},{6,2},{7,3},{8,12},{9,13},{10,... | collective-permute-start | bytes 1572872 | tf_op jit(solution)/shard_map/ppermute | solution.py:32
  31.6 5.9 %collective-permute-start.6 = (bf16[64,1408]{1,0:T(8,128)(2,1)S(1)}, bf16[64,1408]{1,0:T(8,128)(2,1)S(1)}, u32[]{:S(2)}, u32[]{:S(2)}) collective-permute-start(bf16[64,1408]{1,0:T(8,128)(2,1)S(1)} %slice.138), channel_id=1, source_target_pairs={{0,1},{1,0},{2,3},{3,2},{4,5},{5,4},{6,7},{7,6},{8,9},{9,8},{10,11... | collective-permute-start | bytes 540680 | tf_op jit(solution)/shard_map/ppermute | solution.py:32
  32.7 6.9 %collective-permute-start.8 = (bf16[64,1280]{1,0:T(8,128)(2,1)S(1)}, bf16[64,1280]{1,0:T(8,128)(2,1)S(1)}, u32[]{:S(2)}, u32[]{:S(2)}) collective-permute-start(bf16[64,1280]{1,0:T(8,128)(2,1)S(1)} %slice.140), channel_id=1, source_target_pairs={{0,4},{1,5},{2,6},{3,7},{4,0},{5,1},{6,2},{7,3},{8,12},{9,13},{10,... | collective-permute-start | bytes 491528 | tf_op jit(solution)/shard_map/ppermute | solution.py:32
  33.9 5.6 %collective-permute-start.7 = (bf16[64,1408]{1,0:T(8,128)(2,1)S(1)}, bf16[64,1408]{1,0:T(8,128)(2,1)S(1)}, u32[]{:S(2)}, u32[]{:S(2)}) collective-permute-start(bf16[64,1408]{1,0:T(8,128)(2,1)S(1)} %slice.139), channel_id=1, source_target_pairs={{0,3},{1,2},{2,1},{3,0},{4,7},{5,6},{6,5},{7,4},{8,11},{9,10},{10,... | collective-permute-start | bytes 540680 | tf_op jit(solution)/shard_map/ppermute | solution.py:32
  39.6 13.0 %copy-start.12 = (bf16[4096,512]{1,0:T(8,128)(2,1)S(1)}, bf16[4096,512]{1,0:T(8,128)(2,1)}, u32[]{:S(2)}) copy-start(bf16[4096,512]{1,0:T(8,128)(2,1)} %param.20) | copy-start | bytes 12582916
  43.2 5.9 %collective-permute-start.9 = (bf16[272,512]{1,0:T(8,128)(2,1)S(1)}, bf16[272,512]{1,0:T(8,128)(2,1)S(1)}, u32[]{:S(2)}, u32[]{:S(2)}) collective-permute-start(bf16[272,512]{1,0:T(8,128)(2,1)S(1)} %get-tuple-element.36.pay), channel_id=1, source_target_pairs={{0,8},{8,0},{16,24},{24,16},{32,40},{40,32},{48,56},{56,48},{64,72... | collective-permute-start | bytes 835592 | tf_op jit(solution)/shard_map/ppermute | solution.py:36
  49.3 7.1 %collective-permute-start.10 = (bf16[272,256]{1,0:T(8,128)(2,1)S(1)}, bf16[272,256]{1,0:T(8,128)(2,1)S(1)}, u32[]{:S(2)}, u32[]{:S(2)}) collective-permute-start(bf16[272,256]{1,0:T(8,128)(2,1)S(1)} %shard_map.154.chip), channel_id=1, source_target_pairs={{0,16},{8,24},{16,0},{24,8},{32,48},{40,56},{48,32},{56,40},{64,80... | collective-permute-start | bytes 417800 | tf_op jit(solution)/shard_map/ppermute | solution.py:36
  56.4 5.9 %collective-permute-start.11 = (bf16[136,256]{1,0:T(8,128)(2,1)S(1)}, bf16[136,256]{1,0:T(8,128)(2,1)S(1)}, u32[]{:S(2)}, u32[]{:S(2)}) collective-permute-start(bf16[136,256]{1,0:T(8,128)(2,1)S(1)} %get-tuple-element.37), channel_id=1, source_target_pairs={{0,32},{8,40},{16,48},{24,56},{32,64},{40,72},{48,80},{56,88},{64,... | collective-permute-start | bytes 208904 | tf_op jit(solution)/shard_map/ppermute | solution.py:350
  57.7 5.0 %collective-permute-start.12 = (bf16[136,256]{1,0:T(8,128)(2,1)S(1)}, bf16[136,256]{1,0:T(8,128)(2,1)S(1)}, u32[]{:S(2)}, u32[]{:S(2)}) collective-permute-start(bf16[136,256]{1,0:T(8,128)(2,1)S(1)} %get-tuple-element.38), channel_id=1, source_target_pairs={{0,64},{8,72},{16,80},{24,88},{32,96},{40,104},{48,112},{56,120},{... | collective-permute-start | bytes 208904 | tf_op jit(solution)/shard_map/ppermute | solution.py:350
  60.2 4.0 %collective-permute-start.13 = (bf16[136,256]{1,0:T(8,128)(2,1)S(1)}, bf16[136,256]{1,0:T(8,128)(2,1)S(1)}, u32[]{:S(2)}, u32[]{:S(2)}) collective-permute-start(bf16[136,256]{1,0:T(8,128)(2,1)S(1)} %get-tuple-element.39), channel_id=1, source_target_pairs={{0,96},{8,104},{16,112},{24,120},{32,0},{40,8},{48,16},{56,24},{64... | collective-permute-start | bytes 208904 | tf_op jit(solution)/shard_map/ppermute | solution.py:350
  62.3 4.7 %copy-start.4 = (f32[8]{0:T(128)S(1)}, f32[8]{0:T(128)}, u32[]{:S(2)}) copy-start(f32[8]{0:T(128)} %skip_f.3) | copy-start | bytes 100
  62.4 4.7 %copy-start.5 = (f32[8]{0:T(128)S(1)}, f32[8]{0:T(128)}, u32[]{:S(2)}) copy-start(f32[8]{0:T(128)} %skip_r.3) | copy-start | bytes 100
  64.3 7.2 %copy-start.3 = (f32[512]{0:T(512)S(1)}, f32[512]{0:T(512)}, u32[]{:S(2)}) copy-start(f32[512]{0:T(512)} %param.30) | copy-start | bytes 6148
  64.3 7.2 %collective-permute-start.14 = (bf16[256,256]{1,0:T(8,128)(2,1)S(1)}, bf16[256,256]{1,0:T(8,128)(2,1)S(1)}, u32[]{:S(2)}, u32[]{:S(2)}) collective-permute-start(bf16[256,256]{1,0:T(8,128)(2,1)S(1)} %shard_map.156.a), channel_id=1, source_target_pairs={{0,8},{8,0},{16,24},{24,16},{32,40},{40,32},{48,56},{56,48},{64,72... | collective-permute-start | bytes 393224 | tf_op jit(solution)/shard_map/ppermute | solution.py:36
  69.3 6.6 %copy-start.11 = (bf16[512,4096]{1,0:T(8,128)(2,1)S(1)}, bf16[512,4096]{1,0:T(8,128)(2,1)}, u32[]{:S(2)}) copy-start(bf16[512,4096]{1,0:T(8,128)(2,1)} %param.31) | copy-start | bytes 12582916
  72.5 2.7 %collective-permute-start.15 = (f32[8,512]{1,0:T(8,128)S(1)}, f32[8,512]{1,0:T(8,128)S(1)}, u32[]{:S(2)}, u32[]{:S(2)}) collective-permute-start(f32[8,512]{1,0:T(8,128)S(1)} %get-tuple-element.58), channel_id=1, source_target_pairs={{0,1},{1,0},{2,3},{3,2},{4,5},{5,4},{6,7},{7,6},{8,9},{9,8},{10,11... | collective-permute-start | bytes 49160 | tf_op jit(solution)/shard_map/ppermute | solution.py:32
  75.2 3.8 %collective-permute-start.16 = (f32[8,512]{1,0:T(8,128)S(1)}, f32[8,512]{1,0:T(8,128)S(1)}, u32[]{:S(2)}, u32[]{:S(2)}) collective-permute-start(f32[8,512]{1,0:T(8,128)S(1)} %add.47), channel_id=1, source_target_pairs={{0,3},{1,2},{2,1},{3,0},{4,7},{5,6},{6,5},{7,4},{8,11},{9,10},{10,... | collective-permute-start | bytes 49160 | tf_op jit(solution)/shard_map/ppermute | solution.py:32
  79.0 2.6 %collective-permute-start.17 = (f32[8,512]{1,0:T(8,128)S(1)}, f32[8,512]{1,0:T(8,128)S(1)}, u32[]{:S(2)}, u32[]{:S(2)}) collective-permute-start(f32[8,512]{1,0:T(8,128)S(1)} %add.48), channel_id=1, source_target_pairs={{0,4},{1,5},{2,6},{3,7},{4,0},{5,1},{6,2},{7,3},{8,12},{9,13},{10,... | collective-permute-start | bytes 49160 | tf_op jit(solution)/shard_map/ppermute | solution.py:32
  79.1 7.2 %collective-permute-start.21 = (bf16[128,1280]{1,0:T(8,128)(2,1)S(1)}, bf16[128,1280]{1,0:T(8,128)(2,1)S(1)}, u32[]{:S(2)}, u32[]{:S(2)}) collective-permute-start(bf16[128,1280]{1,0:T(8,128)(2,1)S(1)} %slice.154), channel_id=1, source_target_pairs={{0,4},{1,5},{2,6},{3,7},{4,0},{5,1},{6,2},{7,3},{8,12},{9,13},{10,... | collective-permute-start | bytes 983048 | tf_op jit(solution)/shard_map/ppermute | solution.py:32
  80.6 8.3 %collective-permute-start.18 = (bf16[128,1408]{1,0:T(8,128)(2,1)S(1)}, bf16[128,1408]{1,0:T(8,128)(2,1)S(1)}, u32[]{:S(2)}, u32[]{:S(2)}) collective-permute-start(bf16[128,1408]{1,0:T(8,128)(2,1)S(1)} %get-tuple-element.78), channel_id=1, source_target_pairs={{0,3},{1,2},{2,1},{3,0},{4,7},{5,6},{6,5},{7,4},{8,11},{9,10},{10,... | collective-permute-start | bytes 1081352 | tf_op jit(solution)/shard_map/ppermute | solution.py:32
  81.4 7.6 %collective-permute-start.24 = (bf16[128,1408]{1,0:T(8,128)(2,1)S(1)}, bf16[128,1408]{1,0:T(8,128)(2,1)S(1)}, u32[]{:S(2)}, u32[]{:S(2)}) collective-permute-start(bf16[128,1408]{1,0:T(8,128)(2,1)S(1)} %get-tuple-element.79), channel_id=1, source_target_pairs={{0,1},{1,0},{2,3},{3,2},{4,5},{5,4},{6,7},{7,6},{8,9},{9,8},{10,11... | collective-permute-start | bytes 1081352 | tf_op jit(solution)/shard_map/ppermute | solution.py:32
  86.5 14.0 %collective-permute-start.22 = (bf16[64,4096]{1,0:T(8,128)(2,1)S(1)}, bf16[64,4096]{1,0:T(8,128)(2,1)S(1)}, u32[]{:S(2)}, u32[]{:S(2)}) collective-permute-start(bf16[64,4096]{1,0:T(8,128)(2,1)S(1)} %pad_maximum_fusion.2), channel_id=1, source_target_pairs={{0,1},{1,0},{2,3},{3,2},{4,5},{5,4},{6,7},{7,6},{8,9},{9,8},{10,11... | collective-permute-start | bytes 1572872 | tf_op jit(solution)/shard_map/ppermute | solution.py:32
  89.3 12.8 %collective-permute-start.25 = (bf16[64,4096]{1,0:T(8,128)(2,1)S(1)}, bf16[64,4096]{1,0:T(8,128)(2,1)S(1)}, u32[]{:S(2)}, u32[]{:S(2)}) collective-permute-start(bf16[64,4096]{1,0:T(8,128)(2,1)S(1)} %pad_maximum_fusion.3), channel_id=1, source_target_pairs={{0,3},{1,2},{2,1},{3,0},{4,7},{5,6},{6,5},{7,4},{8,11},{9,10},{10,... | collective-permute-start | bytes 1572872 | tf_op jit(solution)/shard_map/ppermute | solution.py:32
  90.5 12.5 %collective-permute-start.19 = (bf16[64,4096]{1,0:T(8,128)(2,1)S(1)}, bf16[64,4096]{1,0:T(8,128)(2,1)S(1)}, u32[]{:S(2)}, u32[]{:S(2)}) collective-permute-start(bf16[64,4096]{1,0:T(8,128)(2,1)S(1)} %pad_maximum_fusion.1), channel_id=1, source_target_pairs={{0,4},{1,5},{2,6},{3,7},{4,0},{5,1},{6,2},{7,3},{8,12},{9,13},{10,... | collective-permute-start | bytes 1572872 | tf_op jit(solution)/shard_map/ppermute | solution.py:32
  100.7 12.7 %collective-permute-start.23 = (bf16[64,4096]{1,0:T(8,128)(2,1)S(1)}, bf16[64,4096]{1,0:T(8,128)(2,1)S(1)}, u32[]{:S(2)}, u32[]{:S(2)}) collective-permute-start(bf16[64,4096]{1,0:T(8,128)(2,1)S(1)} %add_convert_fusion.1), channel_id=1, source_target_pairs={{0,3},{1,2},{2,1},{3,0},{4,7},{5,6},{6,5},{7,4},{8,11},{9,10},{10,... | collective-permute-start | bytes 1572872 | tf_op jit(solution)/shard_map/ppermute | solution.py:32
  102.2 13.1 %collective-permute-start.26 = (bf16[64,4096]{1,0:T(8,128)(2,1)S(1)}, bf16[64,4096]{1,0:T(8,128)(2,1)S(1)}, u32[]{:S(2)}, u32[]{:S(2)}) collective-permute-start(bf16[64,4096]{1,0:T(8,128)(2,1)S(1)} %add_convert_fusion), channel_id=1, source_target_pairs={{0,4},{1,5},{2,6},{3,7},{4,0},{5,1},{6,2},{7,3},{8,12},{9,13},{10,... | collective-permute-start | bytes 1572872 | tf_op jit(solution)/shard_map/ppermute | solution.py:32
  103.2 12.1 %collective-permute-start.20 = (bf16[64,4096]{1,0:T(8,128)(2,1)S(1)}, bf16[64,4096]{1,0:T(8,128)(2,1)S(1)}, u32[]{:S(2)}, u32[]{:S(2)}) collective-permute-start(bf16[64,4096]{1,0:T(8,128)(2,1)S(1)} %add_convert_fusion.2), channel_id=1, source_target_pairs={{0,1},{1,0},{2,3},{3,2},{4,5},{5,4},{6,7},{7,6},{8,9},{9,8},{10,11... | collective-permute-start | bytes 1572872 | tf_op jit(solution)/shard_map/ppermute | solution.py:32
  (8 other events, 8.5 us)
where the time goes:
time: 119 us; the launch traced here: 117 us
  waiting for transfers between devices  50.4 us (42%)
  starting transfers between devices  33.6 us (28%)
  matrix products  13.1 us (11%)
  Pallas kernels  9.27 us (8%)
  local copies, waits for them, and re-layouts  5.55 us (5%)
  other arithmetic  4.61 us (4%)
    ppermute x21, waiting for transfers between devices, over(): return lax.ppermute(array, 'head', [(i, i ^ MASK[dim]) for i in range(8)])  45 us
    ppermute x21, starting transfers between devices, over(): return lax.ppermute(array, 'head', [(i, i ^ MASK[dim]) for i in range(8)])  18.7 us
    dot_general x10, matrix products, dot(): return jnp.dot(a, b, preferred_element_type=f32)  13.1 us
    ppermute x3, starting transfers between devices, along(): return lax.ppermute(array, 'seq', [(i, to(i)) for i in range(16)])  10 us
    ppermute x3, starting transfers between devices, entering_states(): lax.ppermute(sent[k - 1], 'seq', [(i, (i + 4 * k) % 16) for i in range(16)])  4.88 us
    unnamed x31, local copies, waits for them, and re-layouts  4.58 us
    pallas_call x2, Pallas kernels, inside_block(): pl.pallas_call(functools.partial(inside_kernel, block), out_shape=[jax.Sh...  4.46 us
    concatenate x1, other arithmetic, on_device(): jnp.concatenate([w_value, w_bc, jnp.pad(w_step, ((0, 0), (0, STATE - OWN)...  3.67 us
  transfers between devices with their start and end apart: 27, of which 17 were waited for; matrix products, arithmetic and copies ran while one was open for 15% of the time, Pallas kernels for 4%

commit v1 on v0

--- a/solution.py
+++ b/solution.py
@@ -23,7 +23,8 @@
 bf16 = jnp.bfloat16
 
 MASK = {"A": 1, "B": 3, "Z": 4}
-CUT = {"A": (0, 1408), "B": (1408, 2816), "Z": (2816, 4096)}
+LAST = {"B": (0, 2176), "A": (2176, 4096)}
+FIRST = {"A": (0, 2176), "B": (2176, 3584), "Z": (3584, 4096)}
 NEAR, MID, FAR = (1, 3, 4), (2, 7, 5), 6
 SLOTS = (0,) + NEAR + MID + (FAR,)
 
@@ -57,25 +58,25 @@
     return pl.BlockSpec(memory_space=pltpu.SMEM)
 
 
-def norm_kernel(hidden, masked, embed, gain, out):
+def norm_kernel(masked, hidden, embed, gain, out):
     row = lax.broadcasted_iota(jnp.int32, (PIECE, 128), 0)
     flag = jnp.zeros((PIECE, 128), jnp.int32)
     for i in range(PIECE):
         flag = jnp.where(row == i, masked[i], flag)
     source = jnp.where(flag[:, 0:1] == 1, embed[...].astype(f32)[None, :], hidden[...].astype(f32))
     mean = jnp.mean(source * source, axis=1, keepdims=True)
-    out[...] = (source * lax.rsqrt(mean + EPSILON) * gain[...]).astype(bf16)
+    out[...] = (source * lax.rsqrt(mean + EPSILON) * gain[...][None, :]).astype(bf16)
 
 
 def input_norm(hidden, masked, embed, gain):
     return pl.pallas_call(
         norm_kernel,
         out_shape=jax.ShapeDtypeStruct(hidden.shape, bf16),
-        in_specs=[vmem(1)[0], smem()] + vmem(2),
+        in_specs=[smem()] + vmem(3),
         out_specs=vmem(1)[0],
-        compiler_params=budget(6),
+        compiler_params=budget(60),
         name="input_norm",
-    )(hidden, masked, embed, gain[None, :])
+    )(masked, hidden, embed, gain)
 
 
 def softplus(x):
@@ -368,19 +369,19 @@
     at_f = (enter_f, decay[0:1, :] * enter_f + start_f[...])
     at_r = (decay[1:2, :] * enter_r + start_r[...], enter_r)
     ones = jnp.ones((8, WIDE), bf16)
-    pick = lax.broadcasted_iota(jnp.int32, (8, BLOCK), 0)
     for block in range(2):
         span = slice(block * BLOCK, (block + 1) * BLOCK)
         c_blk = c_rows[span, :]
         base_f, base_r, factor_f, factor_r = (inside0, inside1)[block]
-        sums = []
-        for way, (at, base, factor) in enumerate(((at_f, base_f, factor_f), (at_r, base_r, factor_r))):
-            gated = base[...] + dot(c_blk, at[block].astype(bf16)) * factor[...]
-            sums.append(
-                lax.dot_general(ones, (gated * gated).astype(bf16), (((1,), (1,)), ((), ())), preferred_element_type=f32)
+        for way, (state, base, factor) in enumerate(((at_f, base_f, factor_f), (at_r, base_r, factor_r))):
+            gated = base[...] + dot(c_blk, state[block].astype(bf16)) * factor[...]
+            sums = lax.dot_general(
+                ones, (gated * gated).astype(bf16), (((1,), (1,)), ((), ())), preferred_element_type=f32
             )
+            for half in range(2):
+                at = way * 4 + block * 2 + half
+                square[at : at + 1, :] = sums[0:1, half * 128 : (half + 1) * 128]
             gated3[way, 4 * block : 4 * block + 4] = (gated * gain[...]).reshape(4, PIECE, WIDE)
-        square[:, span] = jnp.where(pick == 0, sums[0], sums[1])
     for slot, mask in enumerate(SLOTS):
         at = me ^ mask
         out_f[slot] = gated3[0, at]
@@ -399,7 +400,7 @@
             jax.ShapeDtypeStruct((8, PIECE, WIDE), f32),
             jax.ShapeDtypeStruct((8, PIECE, WIDE), f32),
             jax.ShapeDtypeStruct((2 * PIECE, WIDE), bf16),
-            jax.ShapeDtypeStruct((8, ROWS), f32),
+            jax.ShapeDtypeStruct((8, 128), f32),
         ],
         in_specs=vmem(16),
         out_specs=vmem(4),
@@ -410,16 +411,19 @@
 
 
 def scale_kernel(gated_f, gated_r, square, *refs):
-    outs, scale_out, scale3 = refs[:-2], refs[-2], refs[-1]
+    outs, scale_out, scale3 = refs[:3], refs[3:6], refs[6]
     me = position()[0]
     scale = lax.rsqrt(square[...] / float(HEADS * HEAD_DIM) + EPSILON)
-    padded = jnp.concatenate([scale, jnp.zeros((120, ROWS), f32)], axis=0)
-    scale3[...] = padded.T.reshape(8, PIECE, 128)
+    columns = jnp.concatenate([scale, jnp.zeros((120, 128), f32)], axis=0).T
+    for j in range(4):
+        both = jnp.concatenate([columns[:, j : j + 1], columns[:, 4 + j : 5 + j], jnp.zeros((128, 126), f32)], axis=1)
+        scale3[2 * j : 2 * j + 2] = both.reshape(2, PIECE, 128)
     slot = 0
     for out in outs:
         for i in range(out.shape[0] // PIECE):
             here = scale3[me ^ SLOTS[slot]]
-            scale_out[slot] = here
+            if slot >= 4:
+                scale_out[slot - 4][...] = here
             out[i * PIECE : (i + 1) * PIECE, :] = (
                 gated_f[slot] * here[:, 0:1] + gated_r[slot] * here[:, 1:2]
             ).astype(bf16)
@@ -430,13 +434,31 @@
     return pl.pallas_call(
         scale_kernel,
         out_shape=[jax.ShapeDtypeStruct((n * PIECE, WIDE), bf16) for n in (1, 3, 3)]
-        + [jax.ShapeDtypeStruct((7, PIECE, 128), f32)],
+        + [jax.ShapeDtypeStruct((PIECE, 128), f32)] * 3,
         in_specs=vmem(3),
-        out_specs=vmem(4),
+        out_specs=vmem(6),
         scratch_shapes=[pltpu.VMEM((8, PIECE, 128), f32)],
         compiler_params=budget(10),
         name="scaled_outputs",
     )(gated_f, gated_r, square)
+
+
+def add_part(i, columns, p_mid, arrived, scale):
+    rows, columns = slice(i * PIECE, (i + 1) * PIECE), slice(*columns)
+
+    def kernel(p_mid, arrived, scale, out):
+        out[...] = p_mid[rows, :].astype(bf16)
+        far_f, far_r = arrived[0:PIECE, :].astype(f32), arrived[PIECE : 2 * PIECE, :].astype(f32)
+        far = far_f * scale[:, 0:1] + far_r * scale[:, 1:2]
+        out[:, columns] = (p_mid[rows, columns] + far).astype(bf16)
+
+    return pl.pallas_call(
+        kernel,
+        out_shape=jax.ShapeDtypeStruct((PIECE, p_mid.shape[1]), bf16),
+        in_specs=vmem(3),
+        out_specs=vmem(1)[0],
+        compiler_params=budget(4),
+    )(p_mid, arrived, scale)
 
 
 def on_device(
@@ -462,12 +484,11 @@
     def send(dim, array):
         return over(array, dim)
 
-    at_a, at_b, at_z = [send(dim, own) for dim in "ABZ"]
+    at_a, at_z, at_b = [send(dim, own) for dim in "AZB"]
     at_za = send("Z", at_a)
     at_bz = send("B", at_z)
     at_ab = send("A", at_b)
-    part = lambda array, dim: array[:, slice(*CUT[dim])]
-    far = [send(dim, part(array, dim)) for dim, array in (("A", at_bz), ("B", at_za), ("Z", at_ab))]
+    far = [send(dim, array[:, slice(*LAST[dim])]) for dim, array in (("B", at_za), ("A", at_bz))]
     weights = jnp.concatenate([w_value, w_bc, jnp.pad(w_step, ((0, 0), (0, STATE - OWN)))], axis=1)
     proj, gate = [], []
     for i, blocks in enumerate(((own, at_a, at_b, at_z), (at_ab, at_bz, at_za), far), start=1):
@@ -488,31 +509,26 @@
         mine, his, other, start_f, start_r, decay, c_rows, *inside, out_gain[None, :]
     )
     p_far = dot(far, w_out).astype(bf16)
-    got = {dim: send(dim, part(p_far, dim)) for dim in "ABZ"}
+    got = {dim: send(dim, p_far[:, slice(*FIRST[dim])]) for dim in "ABZ"}
     for dim in "ABZ":
         square = square + send(dim, square)
-    n_own, n_near, n_mid, scale = scaled_outputs(gated_f, gated_r, square)
+    n_own, n_near, n_mid, *scales = scaled_outputs(gated_f, gated_r, square)
     p_mid = dot(n_mid, w_out)
 
     def with_part(mask, dim):
-        i = MID.index(mask)
-        piece, here = p_mid[i * PIECE : (i + 1) * PIECE], scale[4 + i]
-        a, b = CUT[dim]
-        arrived = got[dim].astype(f32)
-        arrived = arrived[:PIECE] * here[:, 0:1] + arrived[PIECE:] * here[:, 1:2]
-        return jnp.concatenate([piece[:, :a], piece[:, a:b] + arrived, piece[:, b:]], axis=1).astype(bf16)
+        return add_part(MID.index(mask), FIRST[dim], p_mid, got[dim], scales[MID.index(mask)])
 
     got_b = send("A", with_part(2, "Z"))
+    got_a = send("Z", with_part(5, "B"))
     got_z = send("B", with_part(7, "A"))
-    got_a = send("Z", with_part(5, "B"))
     p_near = dot(n_near, w_out)
     p_near = lax.optimization_barrier([p_near[i * PIECE : (i + 1) * PIECE] for i in range(3)])
-    total = dot(n_own, w_out)
+    total = lax.optimization_barrier(dot(n_own, w_out))
     near = lambda i, arrived: (p_near[i] + arrived.astype(f32)).astype(bf16)
-    last = [send("A", near(0, got_a)), send("B", near(1, got_b)), send("Z", near(2, got_z))]
-    for arrived in last:
-        total = total + arrived.astype(f32)
-    return total.astype(bf16)
+    total = total + send("Z", near(2, got_z)).astype(f32)
+    total = total + send("A", near(0, got_a)).astype(f32)
+    total = lax.optimization_barrier(total)
+    return (total + send("B", near(1, got_b)).astype(f32)).astype(bf16)
 
 
 def solution(mesh):

time: 119 us -> 122 us (1.025)
  the two profiles are of different devices: /device:TPU:1 before, /device:TPU:0 now
where the time goes in v1:
time: 122 us; the launch traced here: 121 us
  waiting for transfers between devices  60.9 us (50%)
  starting transfers between devices  29.7 us (24%)
  matrix products  12.1 us (10%)
  Pallas kernels  11.2 us (9%)
  other arithmetic  5.08 us (4%)
  local copies, waits for them, and re-layouts  1.95 us (2%)
    ppermute x20, waiting for transfers between devices, over(): return lax.ppermute(array, 'head', [(i, i ^ MASK[dim]) for i in range(8)])  54.8 us
    ppermute x20, starting transfers between devices, over(): return lax.ppermute(array, 'head', [(i, i ^ MASK[dim]) for i in range(8)])  20.2 us
    dot_general x10, matrix products, dot(): return jnp.dot(a, b, preferred_element_type=f32)  12.1 us
    ppermute x3, starting transfers between devices, entering_states(): lax.ppermute(sent[k - 1], 'seq', [(i, (i + 4 * k) % 16) for i in range(16)])  5.71 us
    pallas_call x2, Pallas kernels, inside_block(): pl.pallas_call(functools.partial(inside_kernel, block), out_shape=[jax.Sh...  4.46 us
    ppermute x3, waiting for transfers between devices, along(): return lax.ppermute(array, 'seq', [(i, to(i)) for i in range(16)])  4.28 us
    ppermute x3, starting transfers between devices, along(): return lax.ppermute(array, 'seq', [(i, to(i)) for i in range(16)])  3.84 us
    concatenate x1, other arithmetic, on_device(): jnp.concatenate([w_value, w_bc, jnp.pad(w_step, ((0, 0), (0, STATE - OWN)...  3.71 us
  transfers between devices with their start and end apart: 26, of which 18 were waited for; matrix products, arithmetic and copies ran while one was open for 14% of the time, Pallas kernels for 4%

profile of v1, /device:TPU:0, one launch (start us, length us, event | category | flops | bytes accessed | tf_op | source)
XLA Modules:
  0.0 121.5 jit_solution(12519091634072099619)
XLA Ops:
  0.0 2.2 %input_norm.1 = bf16[64,4096]{1,0:T(8,128)(2,1)} custom-call(s32[64]{0:T(128)} %masked.1, bf16[64,4096]{1,0:T(8,128)(2,1)} %hidden.1, bf16[4096]{0:T(1024)(128)(2,1)} %embed.1, f32[4096]{0:T(1024)} %gain.1), custom_call_target="tpu_custom_call" | custom-call | tf_op jit(solution)/shard_map/input_norm/pallas_call | solution.py:72
  2.2 2.0 %collective-permute-start.2 = (bf16[64,4096]{1,0:T(8,128)(2,1)}, bf16[64,4096]{1,0:T(8,128)(2,1)S(1)}, u32[]{:S(2)}, u32[]{:S(2)}) collective-permute-start(bf16[64,4096]{1,0:T(8,128)(2,1)} %input_norm.1), channel_id=1, source_target_pairs={{0,4},{1,5},{2,6},{3,7},{4,0},{5,1},{6,2},{7,3},{8,12},{9,13},{10,... | collective-permute-start | bytes 1572872 | tf_op jit(solution)/shard_map/ppermute | solution.py:33
  4.3 3.0 %collective-permute-start.1 = (bf16[64,4096]{1,0:T(8,128)(2,1)}, bf16[64,4096]{1,0:T(8,128)(2,1)S(1)}, u32[]{:S(2)}, u32[]{:S(2)}) collective-permute-start(bf16[64,4096]{1,0:T(8,128)(2,1)} %input_norm.1), channel_id=1, source_target_pairs={{0,3},{1,2},{2,1},{3,0},{4,7},{5,6},{6,5},{7,4},{8,11},{9,10},{10,... | collective-permute-start | bytes 1572872 | tf_op jit(solution)/shard_map/ppermute | solution.py:33
  8.7 3.7 %fusion.1 = bf16[4096,896]{1,0:T(8,128)(2,1)S(1)} fusion(bf16[4096,8]{1,0:T(8,128)(2,1)S(1)} %copy.18, bf16[4096,256]{1,0:T(8,128)(2,1)} %param.23, bf16[4096,512]{1,0:T(8,128)(2,1)} %param.21), kind=kLoop, calls=%fused_computation.2 | loop fusion | flops 29360128 | bytes 13697024 | tf_op jit(solution)/shard_map/concatenate | solution.py:492
  12.5 3.9 %collective-permute-done.2 = bf16[64,4096]{1,0:T(8,128)(2,1)S(1)} collective-permute-done((bf16[64,4096]{1,0:T(8,128)(2,1)}, bf16[64,4096]{1,0:T(8,128)(2,1)S(1)}, u32[]{:S(2)}, u32[]{:S(2)}) %collective-permute-start.2) | collective-permute-done | bytes 524320 | tf_op jit(solution)/shard_map/ppermute | solution.py:33
  16.4 3.0 %collective-permute-start.4 = (bf16[64,4096]{1,0:T(8,128)(2,1)S(1)}, bf16[64,4096]{1,0:T(8,128)(2,1)S(1)}, u32[]{:S(2)}, u32[]{:S(2)}) collective-permute-start(bf16[64,4096]{1,0:T(8,128)(2,1)S(1)} %collective-permute-done.2), channel_id=1, source_target_pairs={{0,3},{1,2},{2,1},{3,0},{4,7},{5,6},{6,5},{7,4},{8,11},{9,10},{10,... | collective-permute-start | bytes 1572872 | tf_op jit(solution)/shard_map/ppermute | solution.py:33
  21.3 2.3 %fusion.3.proj1 = f32[256,896]{1,0:T(8,128)S(1)} fusion(bf16[4096,896]{1,0:T(8,128)(2,1)S(1)} %fusion.1, bf16[64,4096]{1,0:T(8,128)(2,1)S(1)} %collective-permute-done.2, bf16[64,4096]{1,0:T(8,128)(2,1)S(1)} %collective-permute-done.1, bf16[64,4096]{1,0:T(8,128)(2,1)S(1)} %collective-permute-done, bf16[64,4096]{1,0:T(8,128)(2,1)S(1)} %copy-done.9), kind=kOutput, calls=%fused_computation.11 | convolution fusion | flops 1887436800 | bytes 10354688 | tf_op jit(solution)/shard_map/dot_general | solution.py:50
  23.6 7.1 %collective-permute-done.4 = bf16[64,4096]{1,0:T(8,128)(2,1)S(1)} collective-permute-done((bf16[64,4096]{1,0:T(8,128)(2,1)S(1)}, bf16[64,4096]{1,0:T(8,128)(2,1)S(1)}, u32[]{:S(2)}, u32[]{:S(2)}) %collective-permute-start.4) | collective-permute-done | bytes 524320 | tf_op jit(solution)/shard_map/ppermute | solution.py:33
  31.0 1.8 %collective-permute-done.5 = bf16[64,4096]{1,0:T(8,128)(2,1)S(1)} collective-permute-done((bf16[64,4096]{1,0:T(8,128)(2,1)S(1)}, bf16[64,4096]{1,0:T(8,128)(2,1)S(1)}, u32[]{:S(2)}, u32[]{:S(2)}) %collective-permute-start.5) | collective-permute-done | bytes 524320 | tf_op jit(solution)/shard_map/ppermute | solution.py:33
  32.9 1.9 %collective-permute-start.6 = (bf16[64,2176]{1,0:T(8,128)(2,1)S(1)}, bf16[64,2176]{1,0:T(8,128)(2,1)S(1)}, u32[]{:S(2)}, u32[]{:S(2)}) collective-permute-start(bf16[64,2176]{1,0:T(8,128)(2,1)S(1)} %slice.32), channel_id=1, source_target_pairs={{0,3},{1,2},{2,1},{3,0},{4,7},{5,6},{6,5},{7,4},{8,11},{9,10},{10,... | collective-permute-start | bytes 835592 | tf_op jit(solution)/shard_map/ppermute | solution.py:33
  34.8 1.8 %fusion.7.proj2 = f32[192,896]{1,0:T(8,128)S(1)} fusion(bf16[192,4096]{1,0:T(8,128)(2,1)S(1)} %constant_dynamic-update-slice_fusion, bf16[4096,896]{1,0:T(8,128)(2,1)S(1)} %fusion.1), kind=kOutput, calls=%fused_computation.20 | convolution fusion | flops 1409286144 | bytes 9601024 | tf_op jit(solution)/shard_map/dot_general | solution.py:50
  36.7 4.0 %collective-permute-done.6 = bf16[64,2176]{1,0:T(8,128)(2,1)S(1)} collective-permute-done((bf16[64,2176]{1,0:T(8,128)(2,1)S(1)}, bf16[64,2176]{1,0:T(8,128)(2,1)S(1)}, u32[]{:S(2)}, u32[]{:S(2)}) %collective-permute-start.6) | collective-permute-done | bytes 278560 | tf_op jit(solution)/shard_map/ppermute | solution.py:33
  42.1 2.2 %piece_states.1 = (bf16[272,512]{1,0:T(8,128)(2,1)S(1)}, bf16[512,512]{1,0:T(8,128)(2,1)S(1)}, bf16[512,128]{1,0:T(8,128)(2,1)S(1)}, bf16[512,128]{1,0:T(8,128)(...) custom-call(f32[256,896]{1,0:T(8,128)S(1)} %fusion.3.proj1, ...), custom_call_target="tpu_custom_call" | custom-call | tf_op jit(solution)/shard_map/piece_states/pallas_call | solution.py:200
  44.5 1.5 %collective-permute-done.8.other.c = bf16[272,512]{1,0:T(8,128)(2,1)S(1)} collective-permute-done((bf16[272,512]{1,0:T(8,128)(2,1)S(1)}, bf16[272,512]{1,0:T(8,128)(2,1)S(1)}, u32[]{:S(2)}, u32[]{:S(2)}) %collective-permute-start.8) | collective-permute-done | bytes 278560 | tf_op jit(solution)/shard_map/ppermute | solution.py:37
  46.1 3.7 %collective-permute-start.9 = (bf16[272,256]{1,0:T(8,128)(2,1)S(1)}, bf16[272,256]{1,0:T(8,128)(2,1)S(1)}, u32[]{:S(2)}, u32[]{:S(2)}) collective-permute-start(bf16[272,256]{1,0:T(8,128)(2,1)S(1)} %shard_map.154.chip), channel_id=1, source_target_pairs={{0,16},{8,24},{16,0},{24,8},{32,48},{40,56},{48,32},{56,40},{64,80... | collective-permute-start | bytes 417800 | tf_op jit(solution)/shard_map/ppermute | solution.py:37
  51.1 2.7 %collective-permute-done.9.beside = bf16[272,256]{1,0:T(8,128)(2,1)S(1)} collective-permute-done((bf16[272,256]{1,0:T(8,128)(2,1)S(1)}, bf16[272,256]{1,0:T(8,128)(2,1)S(1)}, u32[]{:S(2)}, u32[]{:S(2)}) %collective-permute-start.9) | collective-permute-done | bytes 139296 | tf_op jit(solution)/shard_map/ppermute | solution.py:37
  53.9 1.6 %collective-permute-start.10 = (bf16[136,256]{1,0:T(8,128)(2,1)S(1)}, bf16[136,256]{1,0:T(8,128)(2,1)S(1)}, u32[]{:S(2)}, u32[]{:S(2)}) collective-permute-start(bf16[136,256]{1,0:T(8,128)(2,1)S(1)} %get-tuple-element.39), channel_id=1, source_target_pairs={{0,32},{8,40},{16,48},{24,56},{32,64},{40,72},{48,80},{56,88},{64,... | collective-permute-start | bytes 208904 | tf_op jit(solution)/shard_map/ppermute | solution.py:351
  55.4 2.7 %collective-permute-start.11 = (bf16[136,256]{1,0:T(8,128)(2,1)S(1)}, bf16[136,256]{1,0:T(8,128)(2,1)S(1)}, u32[]{:S(2)}, u32[]{:S(2)}) collective-permute-start(bf16[136,256]{1,0:T(8,128)(2,1)S(1)} %get-tuple-element.40), channel_id=1, source_target_pairs={{0,64},{8,72},{16,80},{24,88},{32,96},{40,104},{48,112},{56,120},{... | collective-permute-start | bytes 208904 | tf_op jit(solution)/shard_map/ppermute | solution.py:351
  58.2 1.4 %collective-permute-start.12 = (bf16[136,256]{1,0:T(8,128)(2,1)S(1)}, bf16[136,256]{1,0:T(8,128)(2,1)S(1)}, u32[]{:S(2)}, u32[]{:S(2)}) collective-permute-start(bf16[136,256]{1,0:T(8,128)(2,1)S(1)} %get-tuple-element.41), channel_id=1, source_target_pairs={{0,96},{8,104},{16,112},{24,120},{32,0},{40,8},{48,16},{56,24},{64... | collective-permute-start | bytes 208904 | tf_op jit(solution)/shard_map/ppermute | solution.py:351
  63.6 2.2 %shard_map.158 = (f32[256,512]{1,0:T(8,128)S(1)}, f32[256,512]{1,0:T(8,128)S(1)}, f32[256,512]{1,0:T(8,128)S(1)}, f32[256,512]{1,0:T(8,128)S(1)}) custom-call(f32[256,512]{1,0:T(8,128)S(1)} %fusion.2.gate1, f32[192,512]{1,0:T(8,128)S(1)} %fusion.9.gate2, f32[64,512]{1,0:T(8,128)S(1)} %fusion.10.gate3, bf16[512,512]{1,0:T(8,128)(2,1)S(1)} %get-tuple-element.46.values, ...), custom_call_target="tpu_custom_call" | custom-call | tf_op jit(solution)/shard_map/pallas_call | solution.py:269
  65.8 2.2 %shard_map.157 = (f32[256,512]{1,0:T(8,128)S(1)}, f32[256,512]{1,0:T(8,128)S(1)}, f32[256,512]{1,0:T(8,128)S(1)}, f32[256,512]{1,0:T(8,128)S(1)}) custom-call(f32[256,512]{1,0:T(8,128)S(1)} %fusion.2.gate1, f32[192,512]{1,0:T(8,128)S(1)} %fusion.9.gate2, f32[64,512]{1,0:T(8,128)S(1)} %fusion.10.gate3, bf16[512,512]{1,0:T(8,128)(2,1)S(1)} %get-tuple-element.46.values, ...), custom_call_target="tpu_custom_call" | custom-call | tf_op jit(solution)/shard_map/pallas_call | solution.py:269
  69.1 3.6 %collective-permute-done.14 = f32[8,128]{1,0:T(8,128)S(1)} collective-permute-done((f32[8,128]{1,0:T(8,128)S(1)}, f32[8,128]{1,0:T(8,128)S(1)}, u32[]{:S(2)}, u32[]{:S(2)}) %collective-permute-start.14) | collective-permute-done | bytes 4128 | tf_op jit(solution)/shard_map/ppermute | solution.py:33
  72.7 1.8 %collective-permute-start.15 = (f32[8,128]{1,0:T(8,128)S(1)}, f32[8,128]{1,0:T(8,128)S(1)}, u32[]{:S(2)}, u32[]{:S(2)}) collective-permute-start(f32[8,128]{1,0:T(8,128)S(1)} %add.29), channel_id=1, source_target_pairs={{0,3},{1,2},{2,1},{3,0},{4,7},{5,6},{6,5},{7,4},{8,11},{9,10},{10,... | collective-permute-start | bytes 12296 | tf_op jit(solution)/shard_map/ppermute | solution.py:33
  74.5 3.0 %collective-permute-done.15 = f32[8,128]{1,0:T(8,128)S(1)} collective-permute-done((f32[8,128]{1,0:T(8,128)S(1)}, f32[8,128]{1,0:T(8,128)S(1)}, u32[]{:S(2)}, u32[]{:S(2)}) %collective-permute-start.15) | collective-permute-done | bytes 4128 | tf_op jit(solution)/shard_map/ppermute | solution.py:33
  78.9 1.5 %collective-permute-start.23 = (bf16[128,512]{1,0:T(8,128)(2,1)S(1)}, bf16[128,512]{1,0:T(8,128)(2,1)S(1)}, u32[]{:S(2)}, u32[]{:S(2)}) collective-permute-start(bf16[128,512]{1,0:T(8,128)(2,1)S(1)} %slice.39), channel_id=1, source_target_pairs={{0,4},{1,5},{2,6},{3,7},{4,0},{5,1},{6,2},{7,3},{8,12},{9,13},{10,... | collective-permute-start | bytes 393224 | tf_op jit(solution)/shard_map/ppermute | solution.py:33
  80.4 1.8 %collective-permute-start.20 = (bf16[128,1408]{1,0:T(8,128)(2,1)S(1)}, bf16[128,1408]{1,0:T(8,128)(2,1)S(1)}, u32[]{:S(2)}, u32[]{:S(2)}) collective-permute-start(bf16[128,1408]{1,0:T(8,128)(2,1)S(1)} %slice.38), channel_id=1, source_target_pairs={{0,3},{1,2},{2,1},{3,0},{4,7},{5,6},{6,5},{7,4},{8,11},{9,10},{10,... | collective-permute-start | bytes 1081352 | tf_op jit(solution)/shard_map/ppermute | solution.py:33
  84.8 4.8 %collective-permute-done.20.arrived = bf16[128,1408]{1,0:T(8,128)(2,1)S(1)} collective-permute-done((bf16[128,1408]{1,0:T(8,128)(2,1)S(1)}, bf16[128,1408]{1,0:T(8,128)(2,1)S(1)}, u32[]{:S(2)}, u32[]{:S(2)}) %collective-permute-start.20) | collective-permute-done | bytes 360480 | tf_op jit(solution)/shard_map/ppermute | solution.py:33
  91.8 5.5 %collective-permute-done.17.arrived = bf16[128,2176]{1,0:T(8,128)(2,1)S(1)} collective-permute-done((bf16[128,2176]{1,0:T(8,128)(2,1)S(1)}, bf16[128,2176]{1,0:T(8,128)(2,1)S(1)}, u32[]{:S(2)}, u32[]{:S(2)}) %collective-permute-start.17) | collective-permute-done | bytes 557088 | tf_op jit(solution)/shard_map/ppermute | solution.py:33
  98.9 1.6 %collective-permute-done.21 = bf16[64,4096]{1,0:T(8,128)(2,1)S(1)} collective-permute-done((bf16[64,4096]{1,0:T(8,128)(2,1)S(1)}, bf16[64,4096]{1,0:T(8,128)(2,1)S(1)}, u32[]{:S(2)}, u32[]{:S(2)}) %collective-permute-start.21) | collective-permute-done | bytes 524320 | tf_op jit(solution)/shard_map/ppermute | solution.py:33
  100.7 9.1 %collective-permute-done.18 = bf16[64,4096]{1,0:T(8,128)(2,1)S(1)} collective-permute-done((bf16[64,4096]{1,0:T(8,128)(2,1)S(1)}, bf16[64,4096]{1,0:T(8,128)(2,1)S(1)}, u32[]{:S(2)}, u32[]{:S(2)}) %collective-permute-start.18) | collective-permute-done | bytes 524320 | tf_op jit(solution)/shard_map/ppermute | solution.py:33
  111.0 5.5 %collective-permute-done.22 = bf16[64,4096]{1,0:T(8,128)(2,1)S(1)} collective-permute-done((bf16[64,4096]{1,0:T(8,128)(2,1)S(1)}, bf16[64,4096]{1,0:T(8,128)(2,1)S(1)}, u32[]{:S(2)}, u32[]{:S(2)}) %collective-permute-start.22) | collective-permute-done | bytes 524320 | tf_op jit(solution)/shard_map/ppermute | solution.py:33
  116.6 2.6 %collective-permute-done.19 = bf16[64,4096]{1,0:T(8,128)(2,1)S(1)} collective-permute-done((bf16[64,4096]{1,0:T(8,128)(2,1)S(1)}, bf16[64,4096]{1,0:T(8,128)(2,1)S(1)}, u32[]{:S(2)}, u32[]{:S(2)}) %collective-permute-start.19) | collective-permute-done | bytes 524320 | tf_op jit(solution)/shard_map/ppermute | solution.py:33
  (83 shorter events, 23.0 us)
Async XLA Ops:
  2.2 14.2 %collective-permute-start.2 = (bf16[64,4096]{1,0:T(8,128)(2,1)}, bf16[64,4096]{1,0:T(8,128)(2,1)S(1)}, u32[]{:S(2)}, u32[]{:S(2)}) collective-permute-start(bf16[64,4096]{1,0:T(8,128)(2,1)} %input_norm.1), channel_id=1, source_target_pairs={{0,4},{1,5},{2,6},{3,7},{4,0},{5,1},{6,2},{7,3},{8,12},{9,13},{10,... | collective-permute-start | bytes 1572872 | tf_op jit(solution)/shard_map/ppermute | solution.py:33
  4.3 15.1 %collective-permute-start.1 = (bf16[64,4096]{1,0:T(8,128)(2,1)}, bf16[64,4096]{1,0:T(8,128)(2,1)S(1)}, u32[]{:S(2)}, u32[]{:S(2)}) collective-permute-start(bf16[64,4096]{1,0:T(8,128)(2,1)} %input_norm.1), channel_id=1, source_target_pairs={{0,3},{1,2},{2,1},{3,0},{4,7},{5,6},{6,5},{7,4},{8,11},{9,10},{10,... | collective-permute-start | bytes 1572872 | tf_op jit(solution)/shard_map/ppermute | solution.py:33
  7.3 13.3 %collective-permute-start = (bf16[64,4096]{1,0:T(8,128)(2,1)}, bf16[64,4096]{1,0:T(8,128)(2,1)S(1)}, u32[]{:S(2)}, u32[]{:S(2)}) collective-permute-start(bf16[64,4096]{1,0:T(8,128)(2,1)} %input_norm.1), channel_id=1, source_target_pairs={{0,1},{1,0},{2,3},{3,2},{4,5},{5,4},{6,7},{7,6},{8,9},{9,8},{10,11... | collective-permute-start | bytes 1572872 | tf_op jit(solution)/shard_map/ppermute | solution.py:33
  8.7 12.6 %copy-start.9 = (bf16[64,4096]{1,0:T(8,128)(2,1)S(1)}, bf16[64,4096]{1,0:T(8,128)(2,1)}, u32[]{:S(2)}) copy-start(bf16[64,4096]{1,0:T(8,128)(2,1)} %input_norm.1) | copy-start | bytes 1572868
  16.4 14.3 %collective-permute-start.4 = (bf16[64,4096]{1,0:T(8,128)(2,1)S(1)}, bf16[64,4096]{1,0:T(8,128)(2,1)S(1)}, u32[]{:S(2)}, u32[]{:S(2)}) collective-permute-start(bf16[64,4096]{1,0:T(8,128)(2,1)S(1)} %collective-permute-done.2), channel_id=1, source_target_pairs={{0,3},{1,2},{2,1},{3,0},{4,7},{5,6},{6,5},{7,4},{8,11},{9,10},{10,... | collective-permute-start | bytes 1572872 | tf_op jit(solution)/shard_map/ppermute | solution.py:33
  19.4 15.3 %collective-permute-start.3 = (bf16[64,4096]{1,0:T(8,128)(2,1)S(1)}, bf16[64,4096]{1,0:T(8,128)(2,1)S(1)}, u32[]{:S(2)}, u32[]{:S(2)}) collective-permute-start(bf16[64,4096]{1,0:T(8,128)(2,1)S(1)} %collective-permute-done.1), channel_id=1, source_target_pairs={{0,1},{1,0},{2,3},{3,2},{4,5},{5,4},{6,7},{7,6},{8,9},{9,8},{10,11... | collective-permute-start | bytes 1572872 | tf_op jit(solution)/shard_map/ppermute | solution.py:33
  20.6 12.2 %collective-permute-start.5 = (bf16[64,4096]{1,0:T(8,128)(2,1)S(1)}, bf16[64,4096]{1,0:T(8,128)(2,1)S(1)}, u32[]{:S(2)}, u32[]{:S(2)}) collective-permute-start(bf16[64,4096]{1,0:T(8,128)(2,1)S(1)} %collective-permute-done), channel_id=1, source_target_pairs={{0,4},{1,5},{2,6},{3,7},{4,0},{5,1},{6,2},{7,3},{8,12},{9,13},{10,... | collective-permute-start | bytes 1572872 | tf_op jit(solution)/shard_map/ppermute | solution.py:33
  30.7 10.1 %collective-permute-start.7 = (bf16[64,1920]{1,0:T(8,128)(2,1)S(1)}, bf16[64,1920]{1,0:T(8,128)(2,1)S(1)}, u32[]{:S(2)}, u32[]{:S(2)}) collective-permute-start(bf16[64,1920]{1,0:T(8,128)(2,1)S(1)} %slice.33), channel_id=1, source_target_pairs={{0,1},{1,0},{2,3},{3,2},{4,5},{5,4},{6,7},{7,6},{8,9},{9,8},{10,11... | collective-permute-start | bytes 737288 | tf_op jit(solution)/shard_map/ppermute | solution.py:33
  32.9 7.8 %collective-permute-start.6 = (bf16[64,2176]{1,0:T(8,128)(2,1)S(1)}, bf16[64,2176]{1,0:T(8,128)(2,1)S(1)}, u32[]{:S(2)}, u32[]{:S(2)}) collective-permute-start(bf16[64,2176]{1,0:T(8,128)(2,1)S(1)} %slice.32), channel_id=1, source_target_pairs={{0,3},{1,2},{2,1},{3,0},{4,7},{5,6},{6,5},{7,4},{8,11},{9,10},{10,... | collective-permute-start | bytes 835592 | tf_op jit(solution)/shard_map/ppermute | solution.py:33
  40.8 9.0 %copy-start.8 = (bf16[4096,512]{1,0:T(8,128)(2,1)S(1)}, bf16[4096,512]{1,0:T(8,128)(2,1)}, u32[]{:S(2)}) copy-start(bf16[4096,512]{1,0:T(8,128)(2,1)} %param.20) | copy-start | bytes 12582916
  44.4 1.6 %collective-permute-start.8 = (bf16[272,512]{1,0:T(8,128)(2,1)S(1)}, bf16[272,512]{1,0:T(8,128)(2,1)S(1)}, u32[]{:S(2)}, u32[]{:S(2)}) collective-permute-start(bf16[272,512]{1,0:T(8,128)(2,1)S(1)} %get-tuple-element.38.pay), channel_id=1, source_target_pairs={{0,8},{8,0},{16,24},{24,16},{32,40},{40,32},{48,56},{56,48},{64,72... | collective-permute-start | bytes 835592 | tf_op jit(solution)/shard_map/ppermute | solution.py:37
  46.1 7.6 %collective-permute-start.9 = (bf16[272,256]{1,0:T(8,128)(2,1)S(1)}, bf16[272,256]{1,0:T(8,128)(2,1)S(1)}, u32[]{:S(2)}, u32[]{:S(2)}) collective-permute-start(bf16[272,256]{1,0:T(8,128)(2,1)S(1)} %shard_map.154.chip), channel_id=1, source_target_pairs={{0,16},{8,24},{16,0},{24,8},{32,48},{40,56},{48,32},{56,40},{64,80... | collective-permute-start | bytes 417800 | tf_op jit(solution)/shard_map/ppermute | solution.py:37
  53.9 6.8 %collective-permute-start.10 = (bf16[136,256]{1,0:T(8,128)(2,1)S(1)}, bf16[136,256]{1,0:T(8,128)(2,1)S(1)}, u32[]{:S(2)}, u32[]{:S(2)}) collective-permute-start(bf16[136,256]{1,0:T(8,128)(2,1)S(1)} %get-tuple-element.39), channel_id=1, source_target_pairs={{0,32},{8,40},{16,48},{24,56},{32,64},{40,72},{48,80},{56,88},{64,... | collective-permute-start | bytes 208904 | tf_op jit(solution)/shard_map/ppermute | solution.py:351
  55.4 5.8 %collective-permute-start.11 = (bf16[136,256]{1,0:T(8,128)(2,1)S(1)}, bf16[136,256]{1,0:T(8,128)(2,1)S(1)}, u32[]{:S(2)}, u32[]{:S(2)}) collective-permute-start(bf16[136,256]{1,0:T(8,128)(2,1)S(1)} %get-tuple-element.40), channel_id=1, source_target_pairs={{0,64},{8,72},{16,80},{24,88},{32,96},{40,104},{48,112},{56,120},{... | collective-permute-start | bytes 208904 | tf_op jit(solution)/shard_map/ppermute | solution.py:351
  58.2 4.3 %collective-permute-start.12 = (bf16[136,256]{1,0:T(8,128)(2,1)S(1)}, bf16[136,256]{1,0:T(8,128)(2,1)S(1)}, u32[]{:S(2)}, u32[]{:S(2)}) collective-permute-start(bf16[136,256]{1,0:T(8,128)(2,1)S(1)} %get-tuple-element.41), channel_id=1, source_target_pairs={{0,96},{8,104},{16,112},{24,120},{32,0},{40,8},{48,16},{56,24},{64... | collective-permute-start | bytes 208904 | tf_op jit(solution)/shard_map/ppermute | solution.py:351
  60.6 3.0 %copy-start.1 = (f32[8]{0:T(128)S(1)}, f32[8]{0:T(128)}, u32[]{:S(2)}) copy-start(f32[8]{0:T(128)} %skip_f.3) | copy-start | bytes 100
  60.6 3.0 %copy-start.2 = (f32[8]{0:T(128)S(1)}, f32[8]{0:T(128)}, u32[]{:S(2)}) copy-start(f32[8]{0:T(128)} %skip_r.3) | copy-start | bytes 100
  62.6 5.5 %copy-start = (f32[512]{0:T(512)S(1)}, f32[512]{0:T(512)}, u32[]{:S(2)}) copy-start(f32[512]{0:T(512)} %param.30) | copy-start | bytes 6148
  62.6 5.4 %collective-permute-start.13 = (bf16[256,256]{1,0:T(8,128)(2,1)S(1)}, bf16[256,256]{1,0:T(8,128)(2,1)S(1)}, u32[]{:S(2)}, u32[]{:S(2)}) collective-permute-start(bf16[256,256]{1,0:T(8,128)(2,1)S(1)} %shard_map.156.a), channel_id=1, source_target_pairs={{0,8},{8,0},{16,24},{24,16},{32,40},{40,32},{48,56},{56,48},{64,72... | collective-permute-start | bytes 393224 | tf_op jit(solution)/shard_map/ppermute | solution.py:37
  65.8 12.3 %copy-start.7 = (bf16[512,4096]{1,0:T(8,128)(2,1)S(1)}, bf16[512,4096]{1,0:T(8,128)(2,1)}, u32[]{:S(2)}) copy-start(bf16[512,4096]{1,0:T(8,128)(2,1)} %param.31) | copy-start | bytes 12582916
  69.0 3.7 %collective-permute-start.14 = (f32[8,128]{1,0:T(8,128)S(1)}, f32[8,128]{1,0:T(8,128)S(1)}, u32[]{:S(2)}, u32[]{:S(2)}) collective-permute-start(f32[8,128]{1,0:T(8,128)S(1)} %get-tuple-element.60), channel_id=1, source_target_pairs={{0,1},{1,0},{2,3},{3,2},{4,5},{5,4},{6,7},{7,6},{8,9},{9,8},{10,11... | collective-permute-start | bytes 12296 | tf_op jit(solution)/shard_map/ppermute | solution.py:33
  72.7 4.8 %collective-permute-start.15 = (f32[8,128]{1,0:T(8,128)S(1)}, f32[8,128]{1,0:T(8,128)S(1)}, u32[]{:S(2)}, u32[]{:S(2)}) collective-permute-start(f32[8,128]{1,0:T(8,128)S(1)} %add.29), channel_id=1, source_target_pairs={{0,3},{1,2},{2,1},{3,0},{4,7},{5,6},{6,5},{7,4},{8,11},{9,10},{10,... | collective-permute-start | bytes 12296 | tf_op jit(solution)/shard_map/ppermute | solution.py:33
  77.5 4.7 %collective-permute-start.16 = (f32[8,128]{1,0:T(8,128)S(1)}, f32[8,128]{1,0:T(8,128)S(1)}, u32[]{:S(2)}, u32[]{:S(2)}) collective-permute-start(f32[8,128]{1,0:T(8,128)S(1)} %add.30), channel_id=1, source_target_pairs={{0,4},{1,5},{2,6},{3,7},{4,0},{5,1},{6,2},{7,3},{8,12},{9,13},{10,... | collective-permute-start | bytes 12296 | tf_op jit(solution)/shard_map/ppermute | solution.py:33
  78.9 12.7 %collective-permute-start.23 = (bf16[128,512]{1,0:T(8,128)(2,1)S(1)}, bf16[128,512]{1,0:T(8,128)(2,1)S(1)}, u32[]{:S(2)}, u32[]{:S(2)}) collective-permute-start(bf16[128,512]{1,0:T(8,128)(2,1)S(1)} %slice.39), channel_id=1, source_target_pairs={{0,4},{1,5},{2,6},{3,7},{4,0},{5,1},{6,2},{7,3},{8,12},{9,13},{10,... | collective-permute-start | bytes 393224 | tf_op jit(solution)/shard_map/ppermute | solution.py:33
  80.4 9.2 %collective-permute-start.20 = (bf16[128,1408]{1,0:T(8,128)(2,1)S(1)}, bf16[128,1408]{1,0:T(8,128)(2,1)S(1)}, u32[]{:S(2)}, u32[]{:S(2)}) collective-permute-start(bf16[128,1408]{1,0:T(8,128)(2,1)S(1)} %slice.38), channel_id=1, source_target_pairs={{0,3},{1,2},{2,1},{3,0},{4,7},{5,6},{6,5},{7,4},{8,11},{9,10},{10,... | collective-permute-start | bytes 1081352 | tf_op jit(solution)/shard_map/ppermute | solution.py:33
  82.2 15.1 %collective-permute-start.17 = (bf16[128,2176]{1,0:T(8,128)(2,1)S(1)}, bf16[128,2176]{1,0:T(8,128)(2,1)S(1)}, u32[]{:S(2)}, u32[]{:S(2)}) collective-permute-start(bf16[128,2176]{1,0:T(8,128)(2,1)S(1)} %slice.37), channel_id=1, source_target_pairs={{0,1},{1,0},{2,3},{3,2},{4,5},{5,4},{6,7},{7,6},{8,9},{9,8},{10,11... | collective-permute-start | bytes 1671176 | tf_op jit(solution)/shard_map/ppermute | solution.py:33
  89.8 10.7 %collective-permute-start.21 = (bf16[64,4096]{1,0:T(8,128)(2,1)S(1)}, bf16[64,4096]{1,0:T(8,128)(2,1)S(1)}, u32[]{:S(2)}, u32[]{:S(2)}) collective-permute-start(bf16[64,4096]{1,0:T(8,128)(2,1)S(1)} %shard_map.160), channel_id=1, source_target_pairs={{0,4},{1,5},{2,6},{3,7},{4,0},{5,1},{6,2},{7,3},{8,12},{9,13},{10,... | collective-permute-start | bytes 1572872 | tf_op jit(solution)/shard_map/ppermute | solution.py:33
  91.7 18.2 %collective-permute-start.24 = (bf16[64,4096]{1,0:T(8,128)(2,1)S(1)}, bf16[64,4096]{1,0:T(8,128)(2,1)S(1)}, u32[]{:S(2)}, u32[]{:S(2)}) collective-permute-start(bf16[64,4096]{1,0:T(8,128)(2,1)S(1)} %shard_map.161), channel_id=1, source_target_pairs={{0,1},{1,0},{2,3},{3,2},{4,5},{5,4},{6,7},{7,6},{8,9},{9,8},{10,11... | collective-permute-start | bytes 1572872 | tf_op jit(solution)/shard_map/ppermute | solution.py:33
  97.6 12.2 %collective-permute-start.18 = (bf16[64,4096]{1,0:T(8,128)(2,1)S(1)}, bf16[64,4096]{1,0:T(8,128)(2,1)S(1)}, u32[]{:S(2)}, u32[]{:S(2)}) collective-permute-start(bf16[64,4096]{1,0:T(8,128)(2,1)S(1)} %shard_map.159), channel_id=1, source_target_pairs={{0,3},{1,2},{2,1},{3,0},{4,7},{5,6},{6,5},{7,4},{8,11},{9,10},{10,... | collective-permute-start | bytes 1572872 | tf_op jit(solution)/shard_map/ppermute | solution.py:33
  100.6 16.0 %collective-permute-start.22 = (bf16[64,4096]{1,0:T(8,128)(2,1)S(1)}, bf16[64,4096]{1,0:T(8,128)(2,1)S(1)}, u32[]{:S(2)}, u32[]{:S(2)}) collective-permute-start(bf16[64,4096]{1,0:T(8,128)(2,1)S(1)} %add_convert_fusion.2), channel_id=1, source_target_pairs={{0,1},{1,0},{2,3},{3,2},{4,5},{5,4},{6,7},{7,6},{8,9},{9,8},{10,11... | collective-permute-start | bytes 1572872 | tf_op jit(solution)/shard_map/ppermute | solution.py:33
  109.9 9.3 %collective-permute-start.19 = (bf16[64,4096]{1,0:T(8,128)(2,1)S(1)}, bf16[64,4096]{1,0:T(8,128)(2,1)S(1)}, u32[]{:S(2)}, u32[]{:S(2)}) collective-permute-start(bf16[64,4096]{1,0:T(8,128)(2,1)S(1)} %add_convert_fusion.3), channel_id=1, source_target_pairs={{0,4},{1,5},{2,6},{3,7},{4,0},{5,1},{6,2},{7,3},{8,12},{9,13},{10,... | collective-permute-start | bytes 1572872 | tf_op jit(solution)/shard_map/ppermute | solution.py:33
  110.1 10.5 %collective-permute-start.25 = (bf16[64,4096]{1,0:T(8,128)(2,1)S(1)}, bf16[64,4096]{1,0:T(8,128)(2,1)S(1)}, u32[]{:S(2)}, u32[]{:S(2)}) collective-permute-start(bf16[64,4096]{1,0:T(8,128)(2,1)S(1)} %add_convert_fusion.1), channel_id=1, source_target_pairs={{0,3},{1,2},{2,1},{3,0},{4,7},{5,6},{6,5},{7,4},{8,11},{9,10},{10,... | collective-permute-start | bytes 1572872 | tf_op jit(solution)/shard_map/ppermute | solution.py:33
  (4 other events, 5.5 us)
